TPU v7x, 32 devices: a whole 2x2x4 slice. The times are simulated.
32 devices in a mesh: groups: 2 (over y), sub: 16 (over z, x, core).
Axes of the slice: x: 2, y: 2, z: 4, core: 2. Of those that a mesh axis runs over, the one named last changes fastest.
Arguments:
- modes: bfloat16 [65536, 512], P(('groups', 'sub')), parts along dimension 0, may hold values from -0.5 to 0.5
- eigenvalues: float32 [32, 512], P(('groups', 'sub')), parts along dimension 0, may hold values from 2 to 20
- sub_size: int32 [32], P(('groups', 'sub')), parts along dimension 0, may hold values from 1024 to 2048
- row_offset: int32 [1024, 128], P(('groups', 'sub')), parts along dimension 0, may hold values from 0 to 1023
- stiff_coupling: bfloat16 [1024, 128, 128], P(('groups', 'sub')), parts along dimension 0, may hold values from -0.29882812 to 0.29882812
- iface_offset: int32 [1024], P(('groups', 'sub')), parts along dimension 0, may hold values from 0 to 6
- stiff_iface: float32 [32, 128, 128], P(('groups', 'sub')), parts along dimension 0, may hold values from -18 to 18
- lumped_mass: float32 [32, 128], P(('groups', 'sub')), parts along dimension 0, may hold values from 0.5 to 5
Outputs:
- reduced: float32 [32, 128, 128], P(('groups', 'sub')), parts along dimension 0
- factor: float32 [32, 128, 128], P(('groups', 'sub')), parts along dimension 0
- coupled: bfloat16 [1024, 512, 128], P(('groups', 'sub')), parts along dimension 0
There are 2 independent parts, one for each index of `groups`. A program takes and returns all parts, laid end to end along the dimension named above; each array names one. Nothing has to cross between parts.
Inputs may be any that keep to these rules, and one draw needn't show every extreme that they name: Block b of substructure s belongs to interface (s + iface_offset[b] - 3) mod 16, so a substructure's interfaces lie within 3 places of it in substructure order.
All inputs are finite; a program needn't handle non-finite values.
Results may differ from a plain program's by a relative error of at most 0.001.
The roundings to bfloat16 on the way count: a program that leaves them out, or rounds other values in their place, can miss the bound.
Values sent between devices are 32-bit elements; how exact they have to be, the bound alone decides.
No kernel may reach another device: no remote copies, remote signals or barrier semaphores. Data moves between devices by JAX's collectives and lax.ppermute only.
A program may use at most 64 MiB of HBM per device.

v0:
```python
import jax
import jax.numpy as jnp
from jax import lax
from jax.sharding import PartitionSpec as P

REACH = 3


def passed_along(x, axis, by):
    length = lax.axis_size(axis)
    return lax.ppermute(x, axis, [(i, (i + by) % length) for i in range(length)])


def per_device(
    modes, eigenvalues, sub_size, row_offset, stiff_coupling, iface_offset, stiff_iface, lumped_mass
):
    iface_width = stiff_coupling.shape[2]
    picked_rows = sub_size[0] - 1 - row_offset
    picked = jnp.take(modes, picked_rows, axis=0)
    projected = jnp.einsum(
        "brm,bri->bmi", picked, stiff_coupling, preferred_element_type=jnp.float32
    ).astype(jnp.bfloat16)
    widened = projected.astype(jnp.float32)
    inverse = 1.0 / eigenvalues[0]
    stiff_part = jnp.einsum(
        "bmi,bmj->bij", widened * inverse[None, :, None], widened, precision=lax.Precision.HIGHEST
    )
    mass_part = jnp.einsum(
        "bmi,bmj->bij",
        widened * (inverse * inverse)[None, :, None],
        widened,
        precision=lax.Precision.HIGHEST,
    )
    stacked = jnp.stack([stiff_part, mass_part], axis=1)
    shifted = iface_offset - REACH
    distances = jnp.arange(-REACH, REACH + 1, dtype=jnp.int32)
    selector = (distances[:, None] == shifted[None, :]).astype(jnp.float32)
    by_offset = jnp.einsum("jb,bkxy->jkxy", selector, stacked, precision=lax.Precision.HIGHEST)
    summed = by_offset[REACH]
    for distance in range(-REACH, REACH + 1):
        if distance != 0:
            summed = summed + passed_along(by_offset[distance + REACH], "sub", distance)
    identity = jnp.eye(iface_width, dtype=jnp.float32)
    reduced = stiff_iface - summed[0][None]
    mass_matrix = summed[1][None] + lumped_mass[:, :, None] * identity[None]
    factor = jnp.linalg.cholesky(mass_matrix)
    own_inverse = lax.linalg.triangular_solve(factor[0], identity, left_side=True, lower=True)
    pieces = []
    for distance in range(-REACH, REACH + 1):
        if distance == 0:
            pieces.append(own_inverse)
        else:
            pieces.append(passed_along(own_inverse, "sub", -distance))
    nearby = jnp.stack(pieces)
    chosen = jnp.take(nearby, iface_offset, axis=0)
    solved = jnp.einsum("bmi,bji->bmj", widened, chosen, precision=lax.Precision.HIGHEST)
    return (reduced, factor, solved.astype(jnp.bfloat16))


def solution(mesh):
    placed = (
        P(("groups", "sub"), None),
        P(("groups", "sub"), None),
        P(("groups", "sub")),
        P(("groups", "sub"), None),
        P(("groups", "sub"), None, None),
        P(("groups", "sub")),
        P(("groups", "sub"), None, None),
        P(("groups", "sub"), None),
    )
    return jax.shard_map(
        per_device,
        mesh=mesh,
        in_specs=placed,
        out_specs=(
            P(("groups", "sub"), None, None),
            P(("groups", "sub"), None, None),
            P(("groups", "sub"), None, None),
        ),
        check_vma=False,
    )
```

profile of v0, /device:TPU:1, one launch (start us, length us, event | category | flops | bytes accessed | tf_op | source)
XLA Modules:
  0.0 114.0 jit_solution(12641995247238551872)
XLA Ops:
  0.6 0.0 copy-start
  1.4 0.7 bitcast_clamp_fusion
  2.2 0.7 compare_and_fusion
  2.9 17.3 %gather_fusion = bf16[4096,512]{1,0:T(8,128)(2,1)} fusion(bf16[2048,512]{1,0:T(8,128)(2,1)S(1)} %copy-done, s32[4096]{0:T(1024)S(1)} %bitcast_clamp_fusion), kind=kCustom, calls=%fused_computation | custom fusion | bytes 8404992 | tf_op jit(solution)/shard_map/jit(_take)/gather | solution.py:19
  20.3 6.5 %copy.11 = bf16[32,128,512]{1,2,0:T(8,128)(2,1)} copy(bf16[32,128,512]{2,1,0:T(8,128)(2,1)} %bitcast.61) | data formatting | bytes 8388608 | tf_op jit(solution)/shard_map/jit(_take)/gather | solution.py:19
  26.8 3.4 %fusion.9 = bf16[32,512,128]{2,1,0:T(8,128)(2,1)S(1)} fusion(bf16[32,128,128]{2,1,0:T(8,128)(2,1)S(1)} %copy-done.5, bf16[32,128,512]{1,2,0:T(8,128)(2,1)} %copy.11, pred[32,128]{1,0:T(8,128)(4,1)S(1)} %compare_and_fusion), kind=kOutput, calls=%fused_computation.15 | convolution fusion | flops 541065216 | bytes 9441280 | tf_op jit(solution)/shard_map/brm,bri->bmi/dot_general | solution.py:20
  30.3 7.0 %fusion.15 = f32[32,1,128,128]{3,2,0,1:T(8,128)S(1)} fusion(bf16[32,512,128]{2,1,0:T(8,128)(2,1)S(1)} %fusion.9, f32[512]{0:T(512)S(1)} %bitcast.71), kind=kOutput, calls=%fused_computation.19 | convolution fusion | flops 3225419776 | bytes 6293504 | tf_op jit(solution)/shard_map/bmi,bmj->bij/dot_general | solution.py:25
  37.3 0.0 copy-start.6
  37.3 7.2 %fusion.14 = f32[32,1,128,128]{3,2,0,1:T(8,128)S(1)} fusion(bf16[32,512,128]{2,1,0:T(8,128)(2,1)S(1)} %fusion.9, f32[512]{0:T(512)S(1)} %mul.35), kind=kOutput, calls=%fused_computation.18 | convolution fusion | flops 3225419776 | bytes 6293504 | tf_op jit(solution)/shard_map/bmi,bmj->bij/dot_general | solution.py:28
  44.6 0.3 pad_maximum_fusion
  44.8 0.0 copy-start.2
  44.9 0.0 copy-start.4
  44.9 3.9 %fusion.2 = f32[7,2,128,128]{3,0,2,1:T(8,128)S(1)} fusion(f32[32,2,128,128]{3,2,0,1:T(8,128)S(1)} %pad_maximum_fusion, s32[32]{0:T(128)S(1)} %get-tuple-element.15, s32[7]{0:T(128)S(1)} %iota_add_fusion), kind=kOutput, calls=%fused_computation.7 | convolution fusion | flops 88080608 | bytes 5111964 | tf_op jit(solution)/shard_map/jb,bkxy->jkxy/dot_general | solution.py:38
  48.8 0.7 fusion.28
  49.5 5.7 %collective-permute-start = (f32[2,128,128]{2,1,0:T(8,128)S(1)}, f32[2,128,128]{2,1,0:T(8,128)S(1)}, u32[]{:S(2)}, u32[]{:S(2)}) collective-permute-start(f32[2,128,128]{2,1,0:T(8,128)S(1)} %bitcast.68), channel_id=1, source_target_pairs={{0,13},{1,14},{2,15},{3,0},{4,1},{5,2},{6,3},{7,4},{8,5},{9,6},{10... | collective-permute-start | bytes 393224 | tf_op jit(solution)/shard_map/ppermute | solution.py:11
  55.2 0.3 collective-permute-start.1
  55.5 0.2 collective-permute-start.2
  55.7 1.5 %collective-permute-start.3 = (f32[2,128,128]{2,1,0:T(8,128)S(1)}, f32[2,128,128]{2,1,0:T(8,128)S(1)}, u32[]{:S(2)}, u32[]{:S(2)}) collective-permute-start(f32[2,128,128]{2,1,0:T(8,128)S(1)} %bitcast.65), channel_id=1, source_target_pairs={{0,1},{1,2},{2,3},{3,4},{4,5},{5,6},{6,7},{7,8},{8,9},{9,10},{10,1... | collective-permute-start | bytes 393224 | tf_op jit(solution)/shard_map/ppermute | solution.py:11
  57.2 2.1 %collective-permute-start.4 = (f32[2,128,128]{2,1,0:T(8,128)S(1)}, f32[2,128,128]{2,1,0:T(8,128)S(1)}, u32[]{:S(2)}, u32[]{:S(2)}) collective-permute-start(f32[2,128,128]{2,1,0:T(8,128)S(1)} %bitcast.64), channel_id=1, source_target_pairs={{0,2},{1,3},{2,4},{3,5},{4,6},{5,7},{6,8},{7,9},{8,10},{9,11},{10,... | collective-permute-start | bytes 393224 | tf_op jit(solution)/shard_map/ppermute | solution.py:11
  59.3 0.0 collective-permute-done
  59.3 0.0 collective-permute-start.5
  59.3 2.0 %collective-permute-done.1 = f32[2,128,128]{2,1,0:T(8,128)S(1)} collective-permute-done((f32[2,128,128]{2,1,0:T(8,128)S(1)}, f32[2,128,128]{2,1,0:T(8,128)S(1)}, u32[]{:S(2)}, u32[]{:S(2)}) %collective-permute-start.1) | collective-permute-done | bytes 131104 | tf_op jit(solution)/shard_map/ppermute | solution.py:11
  61.4 0.0 collective-permute-done.2
  61.4 1.4 %collective-permute-done.3 = f32[2,128,128]{2,1,0:T(8,128)S(1)} collective-permute-done((f32[2,128,128]{2,1,0:T(8,128)S(1)}, f32[2,128,128]{2,1,0:T(8,128)S(1)}, u32[]{:S(2)}, u32[]{:S(2)}) %collective-permute-start.3) | collective-permute-done | bytes 131104 | tf_op jit(solution)/shard_map/ppermute | solution.py:11
  62.8 4.2 %collective-permute-done.4 = f32[2,128,128]{2,1,0:T(8,128)S(1)} collective-permute-done((f32[2,128,128]{2,1,0:T(8,128)S(1)}, f32[2,128,128]{2,1,0:T(8,128)S(1)}, u32[]{:S(2)}, u32[]{:S(2)}) %collective-permute-start.4) | collective-permute-done | bytes 131104 | tf_op jit(solution)/shard_map/ppermute | solution.py:11
  67.0 1.2 %collective-permute-done.5 = f32[2,128,128]{2,1,0:T(8,128)S(1)} collective-permute-done((f32[2,128,128]{2,1,0:T(8,128)S(1)}, f32[2,128,128]{2,1,0:T(8,128)S(1)}, u32[]{:S(2)}, u32[]{:S(2)}) %collective-permute-start.5) | collective-permute-done | bytes 131104 | tf_op jit(solution)/shard_map/ppermute | solution.py:11
  68.1 0.1 add_add_fusion
  68.2 0.6 slice_add_fusion
  68.9 0.1 copy.22
  69.0 11.7 %custom-call.7 = f32[1,128,128]{2,1,0:T(8,128)S(1)} custom-call(f32[1,128,128]{2,1,0:T(8,128)S(1)} %fusion.20), custom_call_target="Cholesky" | custom-call | tf_op jit(solution)/shard_map/jit(cholesky)/cholesky | solution.py:46
  80.7 0.6 compare_reduce_fusion
  81.4 1.3 %fusion.21 = (f32[1,128,128]{2,1,0:T(8,128)S(1)}, f32[1,128,128]{2,1,0:T(8,128)}) fusion(f32[1,128,128]{2,1,0:T(8,128)S(1)} %custom-call.7, pred[]{:T(512)} %compare_reduce_fusion), kind=kLoop, calls=%fused_computation.41 | loop fusion | flops 65536 | bytes 196609 | tf_op jit(solution)/shard_map/triangular_solve | solution.py:47
  82.7 9.8 %custom-call.8 = f32[1,128,128]{1,2,0:T(8,128)S(1)} custom-call(f32[1,128,128]{2,1,0:T(8,128)S(1)} %get-tuple-element.3), custom_call_target="InvertDiagBlocksLowerTriangular" | custom-call | tf_op jit(solution)/shard_map/triangular_solve | solution.py:47
  92.5 0.2 fusion.18
  92.7 0.1 collective-permute-start.6
  92.8 1.2 %collective-permute-start.7 = (f32[128,128]{1,0:T(8,128)S(1)}, f32[128,128]{1,0:T(8,128)S(1)}, u32[]{:S(2)}, u32[]{:S(2)}) collective-permute-start(f32[128,128]{1,0:T(8,128)S(1)} %fusion.18), channel_id=1, source_target_pairs={{0,2},{1,3},{2,4},{3,5},{4,6},{5,7},{6,8},{7,9},{8,10},{9,11},{10,... | collective-permute-start | bytes 196616 | tf_op jit(solution)/shard_map/ppermute | solution.py:11
  94.0 1.3 %collective-permute-start.8 = (f32[128,128]{1,0:T(8,128)S(1)}, f32[128,128]{1,0:T(8,128)S(1)}, u32[]{:S(2)}, u32[]{:S(2)}) collective-permute-start(f32[128,128]{1,0:T(8,128)S(1)} %fusion.18), channel_id=1, source_target_pairs={{0,1},{1,2},{2,3},{3,4},{4,5},{5,6},{6,7},{7,8},{8,9},{9,10},{10,1... | collective-permute-start | bytes 196616 | tf_op jit(solution)/shard_map/ppermute | solution.py:11
  95.3 0.0 collective-permute-start.9
  95.3 3.7 %collective-permute-start.10 = (f32[128,128]{1,0:T(8,128)S(1)}, f32[128,128]{1,0:T(8,128)S(1)}, u32[]{:S(2)}, u32[]{:S(2)}) collective-permute-start(f32[128,128]{1,0:T(8,128)S(1)} %fusion.18), channel_id=1, source_target_pairs={{0,14},{1,15},{2,0},{3,1},{4,2},{5,3},{6,4},{7,5},{8,6},{9,7},{10,... | collective-permute-start | bytes 196616 | tf_op jit(solution)/shard_map/ppermute | solution.py:11
  99.0 0.9 collective-permute-done.6
  99.9 2.0 %collective-permute-start.11 = (f32[128,128]{1,0:T(8,128)S(1)}, f32[128,128]{1,0:T(8,128)S(1)}, u32[]{:S(2)}, u32[]{:S(2)}) collective-permute-start(f32[128,128]{1,0:T(8,128)S(1)} %fusion.18), channel_id=1, source_target_pairs={{0,13},{1,14},{2,15},{3,0},{4,1},{5,2},{6,3},{7,4},{8,5},{9,6},{10... | collective-permute-start | bytes 196616 | tf_op jit(solution)/shard_map/ppermute | solution.py:11
  101.9 0.0 collective-permute-done.7
  101.9 0.0 collective-permute-done.8
  102.0 0.0 collective-permute-done.9
  102.0 0.0 collective-permute-done.10
  102.0 2.0 %collective-permute-done.11 = f32[128,128]{1,0:T(8,128)S(1)} collective-permute-done((f32[128,128]{1,0:T(8,128)S(1)}, f32[128,128]{1,0:T(8,128)S(1)}, u32[]{:S(2)}, u32[]{:S(2)}) %collective-permute-start.11) | collective-permute-done | bytes 65568 | tf_op jit(solution)/shard_map/ppermute | solution.py:11
  104.0 2.0 %gather_fusion.1 = f32[32,128,128]{2,1,0:T(8,128)} fusion(f32[7,128,128]{2,1,0:T(8,128)S(1)} %bitcast_dynamic-update-slice_fusion, s32[1024]{0:T(1024)S(1)} %pad_clamp_fusion), kind=kCustom, calls=%fused_computation.1 | custom fusion | bytes 4194432 | tf_op jit(solution)/shard_map/jit(_take)/gather | solution.py:55
  106.0 8.0 %convolution_convert_fusion = bf16[32,512,128]{2,1,0:T(8,128)(2,1)} fusion(bf16[32,512,128]{2,1,0:T(8,128)(2,1)} %copy-done.1, f32[32,128,128]{2,1,0:T(8,128)} %gather_fusion.1, pred[32]{0:T(512)(128)(4,1)S(1)} %compare_and_fusion.1), kind=kOutput, calls=%fused_computation.14 | convolution fusion | flops 3223846912 | bytes 10485792 | tf_op jit(solution)/shard_map/bmi,bji->bmj/dot_general | solution.py:56
  (25 shorter events, 0.1 us)
Async XLA Ops:
  0.6 2.3 %copy-start = (bf16[2048,512]{1,0:T(8,128)(2,1)S(1)}, bf16[2048,512]{1,0:T(8,128)(2,1)}, u32[]{:S(2)}) copy-start(bf16[2048,512]{1,0:T(8,128)(2,1)} %param.8) | copy-start | bytes 6291460
  20.2 6.5 %copy-start.3 = (f32[1,512]{1,0:T(1,128)S(1)}, f32[1,512]{1,0:T(1,128)}, u32[]{:S(2)}) copy-start(f32[1,512]{1,0:T(1,128)} %param.9) | copy-start | bytes 6148
  20.3 6.5 %copy-start.5 = (bf16[32,128,128]{2,1,0:T(8,128)(2,1)S(1)}, bf16[32,128,128]{2,1,0:T(8,128)(2,1)}, u32[]{:S(2)}) copy-start(bf16[32,128,128]{2,1,0:T(8,128)(2,1)} %param.12) | copy-start | bytes 3145732
  30.3 7.1 %copy-start.1 = (bf16[32,512,128]{2,1,0:T(8,128)(2,1)}, bf16[32,512,128]{2,1,0:T(8,128)(2,1)S(1)}, u32[]{:S(2)}) copy-start(bf16[32,512,128]{2,1,0:T(8,128)(2,1)S(1)} %fusion.9) | copy-start | bytes 12582916
  37.3 7.2 %copy-start.6 = (s32[32]{0:T(128)S(1)}, s32[32]{0:T(128)}, u32[]{:S(2)}) copy-start(s32[32]{0:T(128)} %param.13) | copy-start | bytes 388
  44.8 23.4 %copy-start.2 = (f32[1,128,128]{2,1,0:T(8,128)S(1)}, f32[1,128,128]{2,1,0:T(8,128)}, u32[]{:S(2)}) copy-start(f32[1,128,128]{2,1,0:T(8,128)} %param.14) | copy-start | bytes 196612
  44.9 23.4 %copy-start.4 = (f32[1,128]{1,0:T(1,128)S(1)}, f32[1,128]{1,0:T(1,128)}, u32[]{:S(2)}) copy-start(f32[1,128]{1,0:T(1,128)} %param.15) | copy-start | bytes 1540
  49.5 9.8 %collective-permute-start = (f32[2,128,128]{2,1,0:T(8,128)S(1)}, f32[2,128,128]{2,1,0:T(8,128)S(1)}, u32[]{:S(2)}, u32[]{:S(2)}) collective-permute-start(f32[2,128,128]{2,1,0:T(8,128)S(1)} %bitcast.68), channel_id=1, source_target_pairs={{0,13},{1,14},{2,15},{3,0},{4,1},{5,2},{6,3},{7,4},{8,5},{9,6},{10... | collective-permute-start | bytes 393224 | tf_op jit(solution)/shard_map/ppermute | solution.py:11
  55.2 6.2 %collective-permute-start.1 = (f32[2,128,128]{2,1,0:T(8,128)S(1)}, f32[2,128,128]{2,1,0:T(8,128)S(1)}, u32[]{:S(2)}, u32[]{:S(2)}) collective-permute-start(f32[2,128,128]{2,1,0:T(8,128)S(1)} %bitcast.67), channel_id=1, source_target_pairs={{0,14},{1,15},{2,0},{3,1},{4,2},{5,3},{6,4},{7,5},{8,6},{9,7},{10,... | collective-permute-start | bytes 393224 | tf_op jit(solution)/shard_map/ppermute | solution.py:11
  55.5 5.9 %collective-permute-start.2 = (f32[2,128,128]{2,1,0:T(8,128)S(1)}, f32[2,128,128]{2,1,0:T(8,128)S(1)}, u32[]{:S(2)}, u32[]{:S(2)}) collective-permute-start(f32[2,128,128]{2,1,0:T(8,128)S(1)} %bitcast.66), channel_id=1, source_target_pairs={{0,15},{1,0},{2,1},{3,2},{4,3},{5,4},{6,5},{7,6},{8,7},{9,8},{10,9... | collective-permute-start | bytes 393224 | tf_op jit(solution)/shard_map/ppermute | solution.py:11
  55.7 7.1 %collective-permute-start.3 = (f32[2,128,128]{2,1,0:T(8,128)S(1)}, f32[2,128,128]{2,1,0:T(8,128)S(1)}, u32[]{:S(2)}, u32[]{:S(2)}) collective-permute-start(f32[2,128,128]{2,1,0:T(8,128)S(1)} %bitcast.65), channel_id=1, source_target_pairs={{0,1},{1,2},{2,3},{3,4},{4,5},{5,6},{6,7},{7,8},{8,9},{9,10},{10,1... | collective-permute-start | bytes 393224 | tf_op jit(solution)/shard_map/ppermute | solution.py:11
  57.2 9.8 %collective-permute-start.4 = (f32[2,128,128]{2,1,0:T(8,128)S(1)}, f32[2,128,128]{2,1,0:T(8,128)S(1)}, u32[]{:S(2)}, u32[]{:S(2)}) collective-permute-start(f32[2,128,128]{2,1,0:T(8,128)S(1)} %bitcast.64), channel_id=1, source_target_pairs={{0,2},{1,3},{2,4},{3,5},{4,6},{5,7},{6,8},{7,9},{8,10},{9,11},{10,... | collective-permute-start | bytes 393224 | tf_op jit(solution)/shard_map/ppermute | solution.py:11
  59.3 8.8 %collective-permute-start.5 = (f32[2,128,128]{2,1,0:T(8,128)S(1)}, f32[2,128,128]{2,1,0:T(8,128)S(1)}, u32[]{:S(2)}, u32[]{:S(2)}) collective-permute-start(f32[2,128,128]{2,1,0:T(8,128)S(1)} %bitcast.63), channel_id=1, source_target_pairs={{0,3},{1,4},{2,5},{3,6},{4,7},{5,8},{6,9},{7,10},{8,11},{9,12},{10... | collective-permute-start | bytes 393224 | tf_op jit(solution)/shard_map/ppermute | solution.py:11
  92.7 7.2 %collective-permute-start.6 = (f32[128,128]{1,0:T(8,128)S(1)}, f32[128,128]{1,0:T(8,128)S(1)}, u32[]{:S(2)}, u32[]{:S(2)}) collective-permute-start(f32[128,128]{1,0:T(8,128)S(1)} %fusion.18), channel_id=1, source_target_pairs={{0,3},{1,4},{2,5},{3,6},{4,7},{5,8},{6,9},{7,10},{8,11},{9,12},{10... | collective-permute-start | bytes 196616 | tf_op jit(solution)/shard_map/ppermute | solution.py:11
  92.8 9.1 %collective-permute-start.7 = (f32[128,128]{1,0:T(8,128)S(1)}, f32[128,128]{1,0:T(8,128)S(1)}, u32[]{:S(2)}, u32[]{:S(2)}) collective-permute-start(f32[128,128]{1,0:T(8,128)S(1)} %fusion.18), channel_id=1, source_target_pairs={{0,2},{1,3},{2,4},{3,5},{4,6},{5,7},{6,8},{7,9},{8,10},{9,11},{10,... | collective-permute-start | bytes 196616 | tf_op jit(solution)/shard_map/ppermute | solution.py:11
  94.0 8.0 %collective-permute-start.8 = (f32[128,128]{1,0:T(8,128)S(1)}, f32[128,128]{1,0:T(8,128)S(1)}, u32[]{:S(2)}, u32[]{:S(2)}) collective-permute-start(f32[128,128]{1,0:T(8,128)S(1)} %fusion.18), channel_id=1, source_target_pairs={{0,1},{1,2},{2,3},{3,4},{4,5},{5,6},{6,7},{7,8},{8,9},{9,10},{10,1... | collective-permute-start | bytes 196616 | tf_op jit(solution)/shard_map/ppermute | solution.py:11
  95.3 6.7 %collective-permute-start.9 = (f32[128,128]{1,0:T(8,128)S(1)}, f32[128,128]{1,0:T(8,128)S(1)}, u32[]{:S(2)}, u32[]{:S(2)}) collective-permute-start(f32[128,128]{1,0:T(8,128)S(1)} %fusion.18), channel_id=1, source_target_pairs={{0,15},{1,0},{2,1},{3,2},{4,3},{5,4},{6,5},{7,6},{8,7},{9,8},{10,9... | collective-permute-start | bytes 196616 | tf_op jit(solution)/shard_map/ppermute | solution.py:11
  95.3 6.7 %collective-permute-start.10 = (f32[128,128]{1,0:T(8,128)S(1)}, f32[128,128]{1,0:T(8,128)S(1)}, u32[]{:S(2)}, u32[]{:S(2)}) collective-permute-start(f32[128,128]{1,0:T(8,128)S(1)} %fusion.18), channel_id=1, source_target_pairs={{0,14},{1,15},{2,0},{3,1},{4,2},{5,3},{6,4},{7,5},{8,6},{9,7},{10,... | collective-permute-start | bytes 196616 | tf_op jit(solution)/shard_map/ppermute | solution.py:11
  99.9 4.1 %collective-permute-start.11 = (f32[128,128]{1,0:T(8,128)S(1)}, f32[128,128]{1,0:T(8,128)S(1)}, u32[]{:S(2)}, u32[]{:S(2)}) collective-permute-start(f32[128,128]{1,0:T(8,128)S(1)} %fusion.18), channel_id=1, source_target_pairs={{0,13},{1,14},{2,15},{3,0},{4,1},{5,2},{6,3},{7,4},{8,5},{9,6},{10... | collective-permute-start | bytes 196616 | tf_op jit(solution)/shard_map/ppermute | solution.py:11
where the time goes:
time: 114 us
  matrix products  29.8 us (26%)
  local copies, waits for them, and re-layouts  26.8 us (24%)
  other arithmetic  26 us (23%)
  starting transfers between devices  18.1 us (16%)
  waiting for transfers between devices  11.7 us (10%)
  between operations  1.69 us (1%)
    gather x2, local copies, waits for them, and re-layouts, per_device(): picked = jnp.take(modes, picked_rows, axis=0)  23.9 us
    ppermute x12, starting transfers between devices, passed_along(): lax.ppermute(x, axis, [(i, (i + by) % length) for i in range(length)])  18.1 us
    another operation x3, other arithmetic, per_device(): factor = jnp.linalg.cholesky(mass_matrix)  12.4 us
    ppermute x12, waiting for transfers between devices, passed_along(): lax.ppermute(x, axis, [(i, (i + by) % length) for i in range(length)])  11.7 us
    another operation x2, other arithmetic, per_device(): lax.linalg.triangular_solve(factor[0], identity, left_side=True, lower=True)  11.1 us
    dot_general x1, matrix products, per_device(): jnp.einsum('bmi,bji->bmj', widened, chosen, precision=lax.Precision.HIGHEST)  7.96 us
    dot_general x1, matrix products, per_device(): jnp.einsum('bmi,bmj->bij', widened * (inverse * inverse)[None, :, None],...  7.22 us
    dot_general x1, matrix products, per_device(): jnp.einsum('bmi,bmj->bij', widened * inverse[None, :, None], widened, pre...  7.04 us
  transfers between devices with their start and end apart: 12, of which 6 were waited for; matrix products, arithmetic and copies ran while one was open for 0% of the time, Pallas kernels for 0%

commit v1 on v0

v1 whole, which is shorter than its diff:
```python
import jax
import jax.numpy as jnp
from jax import lax
from jax.experimental import pallas as pl
from jax.experimental.pallas import tpu as pltpu
from jax.sharding import PartitionSpec as P

REACH = 3
NEAR = 2 * REACH + 1
GROUP = 4
ROWS = 8
TILE = 16
F32 = jnp.float32
BF16 = jnp.bfloat16
DISTANCES = tuple(d for d in range(-REACH, REACH + 1) if d != 0)


def passed_along(x, axis, by):
    length = lax.axis_size(axis)
    return lax.ppermute(x, axis, [(i, (i + by) % length) for i in range(length)])


def halves(x):
    high = x.astype(BF16)
    return high, (x - high.astype(F32)).astype(BF16)


def dot(a, b, contract=(1, 0)):
    return lax.dot_general(
        a, b, (((contract[0],), (contract[1],)), ((), ())), preferred_element_type=F32
    )


def iotas(shape):
    return (
        lax.broadcasted_iota(jnp.int32, shape, 0),
        lax.broadcasted_iota(jnp.int32, shape, 1),
    )


def project_kernel(
    size, offset, modes, eigen, row_offset, coupling,
    projected, *rest,
):
    packed = rest[:NEAR]
    window, turned, weights, sums, arrived = rest[NEAR:]
    step = pl.program_id(0)
    width = coupling.shape[2]
    picks = coupling.shape[1]
    span = turned.shape[1]

    @pl.when(step == 0)
    def _():
        start = size[0] - span
        base = jnp.minimum(start // TILE * TILE, modes.shape[0] - window.shape[0])
        copy = pltpu.make_async_copy(
            modes.at[pl.ds(pl.multiple_of(base, TILE), window.shape[0]), :], window, arrived
        )
        copy.start()
        sums[...] = jnp.zeros_like(sums)
        inverse = 1.0 / eigen[...]
        weights[0:1, :] = inverse * inverse
        weights[1:2, :] = inverse
        copy.wait()
        moved = pltpu.roll(
            window[...].astype(F32), window.shape[0] - (start - base), 0
        )
        turned[...] = moved[:span].T.astype(BF16)

    place, _ = iotas((span, GROUP * picks))
    wanted = jnp.concatenate(
        [span - 1 - row_offset[pl.ds(step * GROUP + g, 1), :] for g in range(GROUP)], axis=1
    )
    chosen = jnp.where(place == wanted, 1.0, 0.0).astype(BF16)
    picked = dot(turned[...], chosen).astype(BF16)
    for g in range(GROUP):
        mine = picked[:, g * picks : (g + 1) * picks]
        block = dot(mine, coupling[g]).astype(BF16)
        projected[g] = block
        across = dot(coupling[g], mine, (0, 1)).astype(BF16).astype(F32)
        mass = halves(across * weights[0:1, :])
        stiff = halves(across * weights[1:2, :])
        terms = dot(jnp.concatenate([*mass, *stiff], axis=0), block)
        where = offset[step * GROUP + g]
        sums[where, 0] += terms[:width] + terms[width : 2 * width]
        sums[where, 1] += terms[2 * width : 3 * width] + terms[3 * width :]

    @pl.when(step == pl.num_programs(0) - 1)
    def _():
        row, column = iotas((width, width))
        for k in range(NEAR):
            stiff = sums[k, 1]
            packed[k][0:width, :] = jnp.where(row >= column, sums[k, 0], stiff)
            diagonal = jnp.sum(jnp.where(row == column, stiff, 0.0), axis=0, keepdims=True)
            packed[k][width:, :] = jnp.broadcast_to(diagonal, (ROWS, width))


def factor_kernel(*refs):
    received = refs[:NEAR]
    stiff_iface, lumped, reduced, factor, inverse = refs[NEAR:]
    width = lumped.shape[1]
    total = received[0][...]
    for piece in received[1:]:
        total = total + piece[...]
    row, column = iotas((width, width))
    upper = jnp.where(row < column, total[:width], 0.0)
    on_diagonal = jnp.where(row == column, total[width : width + 1, :], 0.0)
    reduced[0] = stiff_iface[0] - (upper + upper.T + on_diagonal)
    lower = jnp.where(row > column, total[:width], 0.0)
    on_diagonal = jnp.where(row == column, total[:width] + lumped[...], 0.0)
    mass = lower + lower.T + on_diagonal
    identity = jnp.where(row == column, 1.0, 0.0)
    panels = width // ROWS
    left = [mass[p * ROWS : (p + 1) * ROWS] for p in range(panels)]
    right = [identity[p * ROWS : (p + 1) * ROWS] for p in range(panels)]
    spread = (ROWS, width)
    for p in range(panels):
        at = p * ROWS
        columns = [
            jnp.broadcast_to(left[p][:, at + j : at + j + 1], spread) for j in range(ROWS)
        ]
        pivot = {
            (i, j): jnp.broadcast_to(columns[j][i : i + 1, :], spread)
            for j in range(ROWS)
            for i in range(j, ROWS)
        }
        scale = []
        for j in range(ROWS):
            scale.append(lax.rsqrt(pivot[j, j]))
            for i in range(j + 1, ROWS):
                pivot[i, j] = pivot[i, j] * scale[j]
            for k in range(j + 1, ROWS):
                for i in range(k, ROWS):
                    pivot[i, k] = pivot[i, k] - pivot[i, j] * pivot[k, j]
        solved_left, solved_right = [], []
        for j in range(ROWS):
            a = jnp.broadcast_to(left[p][j : j + 1, :], spread)
            x = jnp.broadcast_to(right[p][j : j + 1, :], spread)
            for k in range(j):
                a = a - pivot[j, k] * solved_left[k]
                x = x - pivot[j, k] * solved_right[k]
            solved_left.append(a * scale[j])
            solved_right.append(x * scale[j])
        for q in range(p + 1, panels):
            below = []
            for j in range(ROWS):
                v = jnp.broadcast_to(left[q][:, at + j : at + j + 1], spread)
                for k in range(j):
                    v = v - pivot[j, k] * below[k]
                below.append(v * scale[j])
            for j in range(ROWS):
                left[q] = left[q] - below[j] * solved_left[j]
                right[q] = right[q] - below[j] * solved_right[j]
        line, _ = iotas(spread)
        kept_left, kept_right = solved_left[0], solved_right[0]
        for j in range(1, ROWS):
            kept_left = jnp.where(line == j, solved_left[j], kept_left)
            kept_right = jnp.where(line == j, solved_right[j], kept_right)
        left[p], right[p] = kept_left, kept_right
    inverse[...] = jnp.where(row >= column, jnp.concatenate(right, axis=0), 0.0)
    factor[0] = jnp.where(row <= column, jnp.concatenate(left, axis=0), 0.0).T


def transform_kernel(offset, projected, *refs):
    pieces = refs[:NEAR]
    coupled, split = refs[NEAR:]
    step = pl.program_id(0)
    width = projected.shape[2]

    @pl.when(step == 0)
    def _():
        for k in range(NEAR):
            high, low = halves(pieces[k][...])
            split[k, :, 0:width] = high
            split[k, :, width:] = low

    for g in range(GROUP):
        where = offset[step * GROUP + g]
        twice = jnp.concatenate([projected[g], projected[g]], axis=1)
        coupled[g] = dot(twice, split[where], (1, 1)).astype(BF16)


def in_smem():
    return pl.BlockSpec(memory_space=pltpu.SMEM)


def in_vmem():
    return pl.BlockSpec(memory_space=pltpu.VMEM)


def per_device(
    modes, eigenvalues, sub_size, row_offset, stiff_coupling, iface_offset, stiff_iface, lumped_mass
):
    blocks, picks, width = stiff_coupling.shape
    rows, kept = modes.shape
    span = rows // 2
    by_group = pl.BlockSpec((GROUP, kept, width), lambda i: (i, 0, 0))
    projected, *sums = pl.pallas_call(
        project_kernel,
        grid=(blocks // GROUP,),
        in_specs=[
            in_smem(),
            in_smem(),
            pl.BlockSpec(memory_space=pl.ANY),
            in_vmem(),
            in_vmem(),
            pl.BlockSpec((GROUP, picks, width), lambda i: (i, 0, 0)),
        ],
        out_specs=[by_group] + [in_vmem()] * NEAR,
        out_shape=[jax.ShapeDtypeStruct((blocks, kept, width), BF16)]
        + [jax.ShapeDtypeStruct((width + ROWS, width), F32)] * NEAR,
        scratch_shapes=[
            pltpu.VMEM((span + TILE, kept), BF16),
            pltpu.VMEM((kept, span), BF16),
            pltpu.VMEM((8, kept), F32),
            pltpu.VMEM((NEAR, 2, width, width), F32),
            pltpu.SemaphoreType.DMA(()),
        ],
        compiler_params=pltpu.CompilerParams(dimension_semantics=("arbitrary",)),
        name="project",
    )(sub_size, iface_offset, modes, eigenvalues, row_offset, stiff_coupling)
    received = [sums[REACH]] + [passed_along(sums[d + REACH], "sub", d) for d in DISTANCES]
    reduced, factor, inverse = pl.pallas_call(
        factor_kernel,
        in_specs=[in_vmem()] * (NEAR + 2),
        out_specs=[in_vmem()] * 3,
        out_shape=[
            jax.ShapeDtypeStruct((1, width, width), F32),
            jax.ShapeDtypeStruct((1, width, width), F32),
            jax.ShapeDtypeStruct((width, width), F32),
        ],
        name="factor",
    )(*received, stiff_iface, lumped_mass)
    pieces = [
        inverse if d == 0 else passed_along(inverse, "sub", -d) for d in range(-REACH, REACH + 1)
    ]
    coupled = pl.pallas_call(
        transform_kernel,
        grid=(blocks // GROUP,),
        in_specs=[in_smem(), by_group] + [in_vmem()] * NEAR,
        out_specs=by_group,
        out_shape=jax.ShapeDtypeStruct((blocks, kept, width), BF16),
        scratch_shapes=[pltpu.VMEM((NEAR, width, 2 * width), BF16)],
        compiler_params=pltpu.CompilerParams(dimension_semantics=("arbitrary",)),
        name="transform",
    )(iface_offset, projected, *pieces)
    return (reduced, factor, coupled)


def solution(mesh):
    placed = (
        P(("groups", "sub"), None),
        P(("groups", "sub"), None),
        P(("groups", "sub")),
        P(("groups", "sub"), None),
        P(("groups", "sub"), None, None),
        P(("groups", "sub")),
        P(("groups", "sub"), None, None),
        P(("groups", "sub"), None),
    )
    return jax.shard_map(
        per_device,
        mesh=mesh,
        in_specs=placed,
        out_specs=(
            P(("groups", "sub"), None, None),
            P(("groups", "sub"), None, None),
            P(("groups", "sub"), None, None),
        ),
        check_vma=False,
    )
```

time: 114 us -> 66.2 us (0.58)
  Pallas kernels: 0 us -> 35.5 us
  matrix products: 29.8 us -> 0 us
  other arithmetic: 26 us -> 0 us
  local copies, waits for them, and re-layouts: 26.8 us -> 1.22 us
  starting transfers between devices: 18.1 us -> 14 us
  waiting for transfers between devices: 11.7 us -> 13.7 us
    pallas_call x0 -> x3, Pallas kernels: none -> 35.5 us  [the longest x1 21.4 us: per_device(): pl.pallas_call(project_kernel, grid=(blocks // GROUP,), in_specs=[in_smem...]
    dot_general x5 -> x0, matrix products: 29.6 us -> none  [the longest x1 7.96 us: per_device(): jnp.einsum('bmi,bji->bmj', widened, chosen, precision=lax.Precision.HIGHEST)]
    gather x3 -> x0, local copies, waits for them, and re-layouts: 25.9 us -> none  [the longest x2 23.9 us: per_device(): picked = jnp.take(modes, picked_rows, axis=0)]
    another operation x6 -> x0, other arithmetic: 23.8 us -> none  [the longest x3 12.4 us: per_device(): factor = jnp.linalg.cholesky(mass_matrix)]
    ppermute x12, starting transfers between devices: 18.1 us -> 14 us  [passed_along(): lax.ppermute(x, axis, [(i, (i + by) % length) for i in range(length)])]
    ppermute x12, waiting for transfers between devices: 11.7 us -> 13.7 us  [passed_along(): lax.ppermute(x, axis, [(i, (i + by) % length) for i in range(length)])]
  transfers between devices with their start and end apart: 12 -> 12, of which waited for: 6 -> 7; matrix products, arithmetic and copies ran while one was open for 0% -> 0% of each run, Pallas kernels for 0% -> 0%
where the time goes in v1:
time: 66.2 us; the launch traced here: 65.8 us
  Pallas kernels  35.5 us (54%)
  starting transfers between devices  14 us (21%)
  waiting for transfers between devices  13.7 us (21%)
  between operations  1.37 us (2%)
  local copies, waits for them, and re-layouts  1.22 us (2%)
    pallas_call x1, Pallas kernels, per_device(): pl.pallas_call(project_kernel, grid=(blocks // GROUP,), in_specs=[in_smem...  21.4 us
    ppermute x12, starting transfers between devices, passed_along(): lax.ppermute(x, axis, [(i, (i + by) % length) for i in range(length)])  14 us
    ppermute x12, waiting for transfers between devices, passed_along(): lax.ppermute(x, axis, [(i, (i + by) % length) for i in range(length)])  13.7 us
    pallas_call x1, Pallas kernels, per_device(): pl.pallas_call(transform_kernel, grid=(blocks // GROUP,), in_specs=[in_sm...  8.22 us
    pallas_call x1, Pallas kernels, per_device(): pl.pallas_call(factor_kernel, in_specs=[in_vmem()] * (NEAR + 2), out_spec...  5.93 us
  transfers between devices with their start and end apart: 12, of which 7 were waited for; matrix products, arithmetic and copies ran while one was open for 0% of the time, Pallas kernels for 0%

profile of v1, /device:TPU:1, one launch (start us, length us, event | category | flops | bytes accessed | tf_op | source)
XLA Modules:
  0.0 65.8 jit_solution(7461940465723297562)
XLA Ops:
  1.3 21.4 %project.1 = (bf16[32,512,128]{2,1,0:T(8,128)(2,1)}, f32[136,128]{1,0:T(8,128)}, f32[136,128]{1,0:T(8,128)}, f32[136,128]{1,0:T(8,128)}, f32[136,128]{1,0:T(8,12...) custom-call(s32[1]{0:T(128)S(6)} %copy.11.size, s32[32]{0:T(128)} %offset.3, ...), custom_call_target="tpu_custom_call" | custom-call | tf_op jit(solution)/shard_map/project/pallas_call | solution.py:198
  22.6 5.7 %collective-permute-start = (f32[136,128]{1,0:T(8,128)}, f32[136,128]{1,0:T(8,128)S(1)}, u32[]{:S(2)}, u32[]{:S(2)}) collective-permute-start(f32[136,128]{1,0:T(8,128)} %get-tuple-element.15), channel_id=1, source_target_pairs={{0,13},{1,14},{2,15},{3,0},{4,1},{5,2},{6,3},{7,4},{8,5},{9,6},{10... | collective-permute-start | bytes 208904 | tf_op jit(solution)/shard_map/ppermute | solution.py:20
  28.3 0.2 collective-permute-start.1
  28.6 0.2 collective-permute-start.2
  28.8 1.5 %collective-permute-start.3 = (f32[136,128]{1,0:T(8,128)}, f32[136,128]{1,0:T(8,128)S(1)}, u32[]{:S(2)}, u32[]{:S(2)}) collective-permute-start(f32[136,128]{1,0:T(8,128)} %get-tuple-element.18), channel_id=1, source_target_pairs={{0,1},{1,2},{2,3},{3,4},{4,5},{5,6},{6,7},{7,8},{8,9},{9,10},{10,1... | collective-permute-start | bytes 208904 | tf_op jit(solution)/shard_map/ppermute | solution.py:20
  30.3 2.1 %collective-permute-start.4 = (f32[136,128]{1,0:T(8,128)}, f32[136,128]{1,0:T(8,128)S(1)}, u32[]{:S(2)}, u32[]{:S(2)}) collective-permute-start(f32[136,128]{1,0:T(8,128)} %get-tuple-element.19), channel_id=1, source_target_pairs={{0,2},{1,3},{2,4},{3,5},{4,6},{5,7},{6,8},{7,9},{8,10},{9,11},{10,... | collective-permute-start | bytes 208904 | tf_op jit(solution)/shard_map/ppermute | solution.py:20
  32.5 0.0 collective-permute-done.refs_1_
  32.5 0.0 copy-start
  32.5 0.0 collective-permute-start.5
  32.5 0.0 collective-permute-done.1.refs_2_
  32.5 0.0 copy-start.1
  32.5 0.1 collective-permute-done.2.refs_3_
  32.6 0.0 copy-start.2
  32.6 0.0 collective-permute-done.3.refs_4_
  32.6 0.0 copy-start.3
  32.6 5.1 %collective-permute-done.4.refs_5_ = f32[136,128]{1,0:T(8,128)S(1)} collective-permute-done((f32[136,128]{1,0:T(8,128)}, f32[136,128]{1,0:T(8,128)S(1)}, u32[]{:S(2)}, u32[]{:S(2)}) %collective-permute-start.4) | collective-permute-done | bytes 69664 | tf_op jit(solution)/shard_map/ppermute | solution.py:20
  37.7 0.0 copy-start.4
  37.7 1.4 %collective-permute-done.5.refs_6_ = f32[136,128]{1,0:T(8,128)S(1)} collective-permute-done((f32[136,128]{1,0:T(8,128)}, f32[136,128]{1,0:T(8,128)S(1)}, u32[]{:S(2)}, u32[]{:S(2)}) %collective-permute-start.5) | collective-permute-done | bytes 69664 | tf_op jit(solution)/shard_map/ppermute | solution.py:20
  39.1 0.0 copy-start.5
  39.1 0.0 copy-done
  39.1 0.0 copy-done.1
  39.1 0.0 copy-done.2
  39.1 0.0 copy-done.3
  39.1 0.0 copy-done.4
  39.1 0.6 copy-done.5
  39.7 5.9 %factor.1 = (f32[1,128,128]{2,1,0:T(8,128)}, f32[1,128,128]{2,1,0:T(8,128)}, f32[128,128]{1,0:T(8,128)}) custom-call(f32[136,128]{1,0:T(8,128)} %get-tuple-element.14.refs_0_, f32[136,128]{1,0:T(8,128)} %copy-done, f32[136,128]{1,0:T(8,128)} %copy-done.1, f32[136,128]{1,0:T(8,128)} %copy-done.2, f32[136,128]{1,0:T(8,128)} %copy-done.3, ...), custom_call_target="tpu_custom_call" | custom-call | tf_op jit(solution)/shard_map/factor/pallas_call | solution.py:223
  45.7 0.1 collective-permute-start.11
  45.7 0.0 collective-permute-start.10
  45.7 0.5 collective-permute-start.9
  46.3 1.6 %collective-permute-start.8 = (f32[128,128]{1,0:T(8,128)}, f32[128,128]{1,0:T(8,128)S(1)}, u32[]{:S(2)}, u32[]{:S(2)}) collective-permute-start(f32[128,128]{1,0:T(8,128)} %get-tuple-element.24.refs_3_), channel_id=1, source_target_pairs={{0,1},{1,2},{2,3},{3,4},{4,5},{5,6},{6,7},{7,8},{8,9},{9,10},{10,1... | collective-permute-start | bytes 196616 | tf_op jit(solution)/shard_map/ppermute | solution.py:20
  47.9 1.9 %collective-permute-start.7 = (f32[128,128]{1,0:T(8,128)}, f32[128,128]{1,0:T(8,128)S(1)}, u32[]{:S(2)}, u32[]{:S(2)}) collective-permute-start(f32[128,128]{1,0:T(8,128)} %get-tuple-element.24.refs_3_), channel_id=1, source_target_pairs={{0,2},{1,3},{2,4},{3,5},{4,6},{5,7},{6,8},{7,9},{8,10},{9,11},{10,... | collective-permute-start | bytes 196616 | tf_op jit(solution)/shard_map/ppermute | solution.py:20
  49.8 0.5 collective-permute-done.11.refs_6_
  50.3 0.0 collective-permute-start.6
  50.3 0.0 collective-permute-done.10.refs_5_
  50.4 0.0 copy-start.7
  50.4 0.4 collective-permute-done.9.refs_4_
  50.7 0.0 copy-start.8
  50.8 0.0 collective-permute-done.8.refs_2_
  50.8 0.0 copy-start.9
  50.8 4.2 %collective-permute-done.7.refs_1_ = f32[128,128]{1,0:T(8,128)S(1)} collective-permute-done((f32[128,128]{1,0:T(8,128)}, f32[128,128]{1,0:T(8,128)S(1)}, u32[]{:S(2)}, u32[]{:S(2)}) %collective-permute-start.7) | collective-permute-done | bytes 65568 | tf_op jit(solution)/shard_map/ppermute | solution.py:20
  55.0 2.0 %collective-permute-done.6.refs_0_ = f32[128,128]{1,0:T(8,128)S(1)} collective-permute-done((f32[128,128]{1,0:T(8,128)}, f32[128,128]{1,0:T(8,128)S(1)}, u32[]{:S(2)}, u32[]{:S(2)}) %collective-permute-start.6) | collective-permute-done | bytes 65568 | tf_op jit(solution)/shard_map/ppermute | solution.py:20
  56.9 0.0 copy-done.6
  56.9 0.0 copy-done.7
  56.9 0.0 copy-done.8
  57.0 0.0 copy-done.9
  57.0 0.0 copy-done.10
  57.0 0.6 copy-done.11
  57.6 8.2 %transform.1 = bf16[32,512,128]{2,1,0:T(8,128)(2,1)} custom-call(s32[32]{0:T(128)} %offset.3, bf16[32,512,128]{2,1,0:T(8,128)(2,1)} %get-tuple-element.23.projected, f32[128,128]{1,0:T(8,128)} %copy-done.11, f32[128,128]{1,0:T(8,128)} %copy-done.10, f32[128,128]{1,0:T(8,128)} %copy-done.9, f32[128,128]{1,0:T(8,128)} %get-tuple-element.24.refs_3_, ...), custom_call_target="tpu_custom_call" | custom-call | tf_op jit(solution)/shard_map/transform/pallas_call | solution.py:237
  (3 shorter events, 0.0 us)
Async XLA Ops:
  22.6 9.8 %collective-permute-start = (f32[136,128]{1,0:T(8,128)}, f32[136,128]{1,0:T(8,128)S(1)}, u32[]{:S(2)}, u32[]{:S(2)}) collective-permute-start(f32[136,128]{1,0:T(8,128)} %get-tuple-element.15), channel_id=1, source_target_pairs={{0,13},{1,14},{2,15},{3,0},{4,1},{5,2},{6,3},{7,4},{8,5},{9,6},{10... | collective-permute-start | bytes 208904 | tf_op jit(solution)/shard_map/ppermute | solution.py:20
  28.3 4.1 %collective-permute-start.1 = (f32[136,128]{1,0:T(8,128)}, f32[136,128]{1,0:T(8,128)S(1)}, u32[]{:S(2)}, u32[]{:S(2)}) collective-permute-start(f32[136,128]{1,0:T(8,128)} %get-tuple-element.16), channel_id=1, source_target_pairs={{0,14},{1,15},{2,0},{3,1},{4,2},{5,3},{6,4},{7,5},{8,6},{9,7},{10,... | collective-permute-start | bytes 208904 | tf_op jit(solution)/shard_map/ppermute | solution.py:20
  28.6 4.0 %collective-permute-start.2 = (f32[136,128]{1,0:T(8,128)}, f32[136,128]{1,0:T(8,128)S(1)}, u32[]{:S(2)}, u32[]{:S(2)}) collective-permute-start(f32[136,128]{1,0:T(8,128)} %get-tuple-element.17), channel_id=1, source_target_pairs={{0,15},{1,0},{2,1},{3,2},{4,3},{5,4},{6,5},{7,6},{8,7},{9,8},{10,9... | collective-permute-start | bytes 208904 | tf_op jit(solution)/shard_map/ppermute | solution.py:20
  28.8 3.8 %collective-permute-start.3 = (f32[136,128]{1,0:T(8,128)}, f32[136,128]{1,0:T(8,128)S(1)}, u32[]{:S(2)}, u32[]{:S(2)}) collective-permute-start(f32[136,128]{1,0:T(8,128)} %get-tuple-element.18), channel_id=1, source_target_pairs={{0,1},{1,2},{2,3},{3,4},{4,5},{5,6},{6,7},{7,8},{8,9},{9,10},{10,1... | collective-permute-start | bytes 208904 | tf_op jit(solution)/shard_map/ppermute | solution.py:20
  30.3 7.3 %collective-permute-start.4 = (f32[136,128]{1,0:T(8,128)}, f32[136,128]{1,0:T(8,128)S(1)}, u32[]{:S(2)}, u32[]{:S(2)}) collective-permute-start(f32[136,128]{1,0:T(8,128)} %get-tuple-element.19), channel_id=1, source_target_pairs={{0,2},{1,3},{2,4},{3,5},{4,6},{5,7},{6,8},{7,9},{8,10},{9,11},{10,... | collective-permute-start | bytes 208904 | tf_op jit(solution)/shard_map/ppermute | solution.py:20
  32.5 6.6 %copy-start = (f32[136,128]{1,0:T(8,128)}, f32[136,128]{1,0:T(8,128)S(1)}, u32[]{:S(2)}) copy-start(f32[136,128]{1,0:T(8,128)S(1)} %collective-permute-done.refs_1_) | copy-start | bytes 208900
  32.5 6.6 %collective-permute-start.5 = (f32[136,128]{1,0:T(8,128)}, f32[136,128]{1,0:T(8,128)S(1)}, u32[]{:S(2)}, u32[]{:S(2)}) collective-permute-start(f32[136,128]{1,0:T(8,128)} %get-tuple-element.20), channel_id=1, source_target_pairs={{0,3},{1,4},{2,5},{3,6},{4,7},{5,8},{6,9},{7,10},{8,11},{9,12},{10... | collective-permute-start | bytes 208904 | tf_op jit(solution)/shard_map/ppermute | solution.py:20
  32.5 6.6 %copy-start.1 = (f32[136,128]{1,0:T(8,128)}, f32[136,128]{1,0:T(8,128)S(1)}, u32[]{:S(2)}) copy-start(f32[136,128]{1,0:T(8,128)S(1)} %collective-permute-done.1.refs_2_) | copy-start | bytes 208900
  32.6 6.6 %copy-start.2 = (f32[136,128]{1,0:T(8,128)}, f32[136,128]{1,0:T(8,128)S(1)}, u32[]{:S(2)}) copy-start(f32[136,128]{1,0:T(8,128)S(1)} %collective-permute-done.2.refs_3_) | copy-start | bytes 208900
  32.6 6.6 %copy-start.3 = (f32[136,128]{1,0:T(8,128)}, f32[136,128]{1,0:T(8,128)S(1)}, u32[]{:S(2)}) copy-start(f32[136,128]{1,0:T(8,128)S(1)} %collective-permute-done.3.refs_4_) | copy-start | bytes 208900
  37.7 1.5 %copy-start.4 = (f32[136,128]{1,0:T(8,128)}, f32[136,128]{1,0:T(8,128)S(1)}, u32[]{:S(2)}) copy-start(f32[136,128]{1,0:T(8,128)S(1)} %collective-permute-done.4.refs_5_) | copy-start | bytes 208900
  39.1 0.6 copy-start.5
  45.7 4.7 %collective-permute-start.11 = (f32[128,128]{1,0:T(8,128)}, f32[128,128]{1,0:T(8,128)S(1)}, u32[]{:S(2)}, u32[]{:S(2)}) collective-permute-start(f32[128,128]{1,0:T(8,128)} %get-tuple-element.24.refs_3_), channel_id=1, source_target_pairs={{0,13},{1,14},{2,15},{3,0},{4,1},{5,2},{6,3},{7,4},{8,5},{9,6},{10... | collective-permute-start | bytes 196616 | tf_op jit(solution)/shard_map/ppermute | solution.py:20
  45.7 4.6 %collective-permute-start.10 = (f32[128,128]{1,0:T(8,128)}, f32[128,128]{1,0:T(8,128)S(1)}, u32[]{:S(2)}, u32[]{:S(2)}) collective-permute-start(f32[128,128]{1,0:T(8,128)} %get-tuple-element.24.refs_3_), channel_id=1, source_target_pairs={{0,14},{1,15},{2,0},{3,1},{4,2},{5,3},{6,4},{7,5},{8,6},{9,7},{10,... | collective-permute-start | bytes 196616 | tf_op jit(solution)/shard_map/ppermute | solution.py:20
  45.7 5.0 %collective-permute-start.9 = (f32[128,128]{1,0:T(8,128)}, f32[128,128]{1,0:T(8,128)S(1)}, u32[]{:S(2)}, u32[]{:S(2)}) collective-permute-start(f32[128,128]{1,0:T(8,128)} %get-tuple-element.24.refs_3_), channel_id=1, source_target_pairs={{0,15},{1,0},{2,1},{3,2},{4,3},{5,4},{6,5},{7,6},{8,7},{9,8},{10,9... | collective-permute-start | bytes 196616 | tf_op jit(solution)/shard_map/ppermute | solution.py:20
  46.3 4.5 %collective-permute-start.8 = (f32[128,128]{1,0:T(8,128)}, f32[128,128]{1,0:T(8,128)S(1)}, u32[]{:S(2)}, u32[]{:S(2)}) collective-permute-start(f32[128,128]{1,0:T(8,128)} %get-tuple-element.24.refs_3_), channel_id=1, source_target_pairs={{0,1},{1,2},{2,3},{3,4},{4,5},{5,6},{6,7},{7,8},{8,9},{9,10},{10,1... | collective-permute-start | bytes 196616 | tf_op jit(solution)/shard_map/ppermute | solution.py:20
  47.9 7.1 %collective-permute-start.7 = (f32[128,128]{1,0:T(8,128)}, f32[128,128]{1,0:T(8,128)S(1)}, u32[]{:S(2)}, u32[]{:S(2)}) collective-permute-start(f32[128,128]{1,0:T(8,128)} %get-tuple-element.24.refs_3_), channel_id=1, source_target_pairs={{0,2},{1,3},{2,4},{3,5},{4,6},{5,7},{6,8},{7,9},{8,10},{9,11},{10,... | collective-permute-start | bytes 196616 | tf_op jit(solution)/shard_map/ppermute | solution.py:20
  50.3 6.6 %copy-start.6 = (f32[128,128]{1,0:T(8,128)}, f32[128,128]{1,0:T(8,128)S(1)}, u32[]{:S(2)}) copy-start(f32[128,128]{1,0:T(8,128)S(1)} %collective-permute-done.11.refs_6_) | copy-start | bytes 196612
  50.3 6.6 %collective-permute-start.6 = (f32[128,128]{1,0:T(8,128)}, f32[128,128]{1,0:T(8,128)S(1)}, u32[]{:S(2)}, u32[]{:S(2)}) collective-permute-start(f32[128,128]{1,0:T(8,128)} %get-tuple-element.24.refs_3_), channel_id=1, source_target_pairs={{0,3},{1,4},{2,5},{3,6},{4,7},{5,8},{6,9},{7,10},{8,11},{9,12},{10... | collective-permute-start | bytes 196616 | tf_op jit(solution)/shard_map/ppermute | solution.py:20
  50.4 6.6 %copy-start.7 = (f32[128,128]{1,0:T(8,128)}, f32[128,128]{1,0:T(8,128)S(1)}, u32[]{:S(2)}) copy-start(f32[128,128]{1,0:T(8,128)S(1)} %collective-permute-done.10.refs_5_) | copy-start | bytes 196612
  50.7 6.2 %copy-start.8 = (f32[128,128]{1,0:T(8,128)}, f32[128,128]{1,0:T(8,128)S(1)}, u32[]{:S(2)}) copy-start(f32[128,128]{1,0:T(8,128)S(1)} %collective-permute-done.9.refs_4_) | copy-start | bytes 196612
  50.8 6.2 %copy-start.9 = (f32[128,128]{1,0:T(8,128)}, f32[128,128]{1,0:T(8,128)S(1)}, u32[]{:S(2)}) copy-start(f32[128,128]{1,0:T(8,128)S(1)} %collective-permute-done.8.refs_2_) | copy-start | bytes 196612
  55.0 2.0 %copy-start.10 = (f32[128,128]{1,0:T(8,128)}, f32[128,128]{1,0:T(8,128)S(1)}, u32[]{:S(2)}) copy-start(f32[128,128]{1,0:T(8,128)S(1)} %collective-permute-done.7.refs_1_) | copy-start | bytes 196612
  56.9 0.6 copy-start.11

commit v2 on v1

v2 whole, which is shorter than its diff:
```python
import jax
import jax.numpy as jnp
from jax import lax
from jax.experimental import pallas as pl
from jax.experimental.pallas import tpu as pltpu
from jax.sharding import PartitionSpec as P

REACH = 3
NEAR = 2 * REACH + 1
GROUP = 4
ROWS = 8
PARTS = 4
TILE = 16
VMEM_LIMIT = 24 << 20
F32 = jnp.float32
BF16 = jnp.bfloat16
DISTANCES = tuple(d for d in range(-REACH, REACH + 1) if d != 0)


def passed_along(x, axis, by):
    length = lax.axis_size(axis)
    moved = lax.ppermute(x, axis, [(i, (i + by) % length) for i in range(length)])
    return pltpu.with_memory_space_constraint(moved, pltpu.VMEM)


def halves(x):
    high = x.astype(BF16)
    return high, (x - high.astype(F32)).astype(BF16)


def dot(a, b, contract=(1, 0)):
    return lax.dot_general(
        a, b, (((contract[0],), (contract[1],)), ((), ())), preferred_element_type=F32
    )


def iotas(shape):
    return (
        lax.broadcasted_iota(jnp.int32, shape, 0),
        lax.broadcasted_iota(jnp.int32, shape, 1),
    )


def project_kernel(size, offset, modes, eigen, row_offset, coupling, turned, *rest):
    packed = rest[:NEAR]
    offsets, rows, values, wants, blocks_in, span_rows, picked, sums, arrived = rest[NEAR:]
    blocks, picks, width = coupling.shape
    span = span_rows.shape[0]
    part = rows.shape[0] // PARTS
    pairs = [(row_offset, wants), (offset, offsets), (eigen, values)]
    pairs += [
        (modes.at[pl.ds(k * part, part), :], rows.at[pl.ds(k * part, part), :])
        for k in range(PARTS)
    ]
    pairs.append((coupling, blocks_in))
    copies = [
        pltpu.make_async_copy(source, target, arrived.at[k])
        for k, (source, target) in enumerate(pairs)
    ]
    for copy in copies:
        copy.start()
    sums[...] = jnp.zeros_like(sums)
    _, place = iotas((picks, span))
    for copy in copies[:3]:
        copy.wait()
    wanted = (span - 1 - wants[...]).T
    inverse = 1.0 / values[...]
    weight = inverse * inverse
    start = size[0] - span
    base = jnp.minimum(start // TILE * TILE, rows.shape[0] - span - TILE)
    for copy in copies[3:]:
        copy.wait()
    window = rows[pl.ds(pl.multiple_of(base, TILE), span + TILE), :].astype(F32)
    moved = pltpu.roll(window, span + TILE - (start - base), 0)
    span_rows[...] = moved[:span].astype(BF16)
    groups = blocks // GROUP
    for i in range(groups + 2):
        if i >= 2:
            for b in range((i - 2) * GROUP, (i - 1) * GROUP):
                block = turned[b]
                mass = halves(block.astype(F32) * weight)
                terms = dot(jnp.concatenate(mass, axis=0), block, (1, 1))
                sums[offsets[b]] += terms[:width] + terms[width:]
        if 1 <= i <= groups:
            for g in range(GROUP):
                b = (i - 1) * GROUP + g
                mine = picked[(i - 1) % 2, g * picks : (g + 1) * picks, :]
                turned[b] = dot(blocks_in[b].T, mine).astype(BF16)
        if i < groups:
            chosen = [
                jnp.where(place == wanted[:, b : b + 1], 1.0, 0.0).astype(BF16)
                for b in range(i * GROUP, (i + 1) * GROUP)
            ]
            picked[i % 2] = dot(jnp.concatenate(chosen, axis=0), span_rows[...]).astype(BF16)
    for k in range(NEAR):
        packed[k][...] = sums[k]


def stiffen_kernel(offset, eigen, turned, projected, sums):
    width = sums.shape[1]
    sums[...] = jnp.zeros_like(sums)
    weight = 1.0 / eigen[...]
    for b in range(turned.shape[0]):
        block = turned[b]
        stiff = halves(block.astype(F32) * weight)
        terms = dot(jnp.concatenate(stiff, axis=0), block, (1, 1))
        sums[offset[b]] += terms[:width] + terms[width:]
        projected[b] = block.T


def factor_kernel(*refs):
    received = refs[:NEAR]
    lumped, stiff, factor = refs[NEAR : NEAR + 3]
    parcels = refs[NEAR + 3 :]
    width = lumped.shape[1]
    total = received[0][...]
    for piece in received[1:]:
        total = total + piece[...]
    row, column = iotas((width, width))
    lower = jnp.where(row > column, total, 0.0)
    mass = lower + lower.T + jnp.where(row == column, total + lumped[...], 0.0)
    identity = jnp.where(row == column, 1.0, 0.0)
    panels = width // ROWS
    left = [mass[p * ROWS : (p + 1) * ROWS] for p in range(panels)]
    right = [identity[p * ROWS : (p + 1) * ROWS] for p in range(panels)]
    spread = (ROWS, width)
    for p in range(panels):
        at = p * ROWS
        columns = [
            jnp.broadcast_to(left[p][:, at + j : at + j + 1], spread) for j in range(ROWS)
        ]
        pivot = {
            (i, j): jnp.broadcast_to(columns[j][i : i + 1, :], spread)
            for j in range(ROWS)
            for i in range(j, ROWS)
        }
        scale = []
        for j in range(ROWS):
            scale.append(lax.rsqrt(pivot[j, j]))
            for i in range(j + 1, ROWS):
                pivot[i, j] = pivot[i, j] * scale[j]
            for k in range(j + 1, ROWS):
                for i in range(k, ROWS):
                    pivot[i, k] = pivot[i, k] - pivot[i, j] * pivot[k, j]
        solved_left, solved_right = [], []
        for j in range(ROWS):
            a = jnp.broadcast_to(left[p][j : j + 1, :], spread)
            x = jnp.broadcast_to(right[p][j : j + 1, :], spread)
            for k in range(j):
                a = a - pivot[j, k] * solved_left[k]
                x = x - pivot[j, k] * solved_right[k]
            solved_left.append(a * scale[j])
            solved_right.append(x * scale[j])
        for q in range(p + 1, panels):
            below = []
            for j in range(ROWS):
                v = jnp.broadcast_to(left[q][:, at + j : at + j + 1], spread)
                for k in range(j):
                    v = v - pivot[j, k] * below[k]
                below.append(v * scale[j])
            for j in range(ROWS):
                left[q] = left[q] - below[j] * solved_left[j]
                right[q] = right[q] - below[j] * solved_right[j]
        line, _ = iotas(spread)
        kept_left, kept_right = solved_left[0], solved_right[0]
        for j in range(1, ROWS):
            kept_left = jnp.where(line == j, solved_left[j], kept_left)
            kept_right = jnp.where(line == j, solved_right[j], kept_right)
        left[p], right[p] = kept_left, kept_right
    inverse = jnp.concatenate(right, axis=0)
    for k in range(NEAR):
        parcels[k][0:width, :] = jnp.where(row >= column, inverse, stiff[k])
        diagonal = jnp.sum(jnp.where(row == column, stiff[k], 0.0), axis=0, keepdims=True)
        parcels[k][width:, :] = jnp.broadcast_to(diagonal, (ROWS, width))
    factor[0] = jnp.where(row <= column, jnp.concatenate(left, axis=0), 0.0).T


def transform_kernel(offset, projected, stiff_iface, *refs):
    parcels = refs[:NEAR]
    reduced, coupled, split, held, sent = refs[NEAR:]
    blocks, kept, width = projected.shape
    row, column = iotas((width, width))
    upper = jnp.zeros((width, width), F32)
    diagonal = jnp.zeros((1, width), F32)
    for k in range(NEAR):
        piece = parcels[k][0:width, :]
        high, low = halves(jnp.where(row >= column, piece, 0.0))
        split[k, :, 0:width] = high
        split[k, :, width:] = low
        upper = upper + jnp.where(row < column, piece, 0.0)
        diagonal = diagonal + parcels[k][width : width + 1, :]
    copies = []
    for first in range(0, blocks, GROUP):
        for b in range(first, first + GROUP):
            twice = jnp.concatenate([projected[b], projected[b]], axis=1)
            held[b] = dot(twice, split[offset[b]], (1, 1)).astype(BF16)
        some = pl.ds(first, GROUP)
        copies.append(
            pltpu.make_async_copy(held.at[some], coupled.at[some], sent.at[first // GROUP])
        )
        copies[-1].start()
    on_diagonal = jnp.where(row == column, diagonal, 0.0)
    reduced[0] = stiff_iface[0] - (upper + upper.T + on_diagonal)
    for copy in copies:
        copy.wait()


def in_smem():
    return pl.BlockSpec(memory_space=pltpu.SMEM)


def in_vmem():
    return pl.BlockSpec(memory_space=pltpu.VMEM)


def per_device(
    modes, eigenvalues, sub_size, row_offset, stiff_coupling, iface_offset, stiff_iface, lumped_mass
):
    blocks, picks, width = stiff_coupling.shape
    rows, kept = modes.shape
    span = rows // 2
    def array(*shape, dtype=F32):
        return jax.ShapeDtypeStruct(shape, dtype)

    def near(*shape, dtype=F32):
        return pltpu.VMEM(shape, dtype)

    anywhere = pl.BlockSpec(memory_space=pl.ANY)
    turned, *sums = pl.pallas_call(
        project_kernel,
        in_specs=[in_smem()] + [pl.BlockSpec(memory_space=pltpu.HBM)] * 5,
        out_specs=[in_vmem()] * (1 + NEAR),
        out_shape=[near(blocks, width, kept, dtype=BF16)] + [near(width, width)] * NEAR,
        scratch_shapes=[
            pltpu.SMEM(iface_offset.shape, jnp.int32),
            pltpu.VMEM(modes.shape, BF16),
            pltpu.VMEM(eigenvalues.shape, F32),
            pltpu.VMEM(row_offset.shape, jnp.int32),
            pltpu.VMEM(stiff_coupling.shape, BF16),
            pltpu.VMEM((span, kept), BF16),
            pltpu.VMEM((2, GROUP * picks, kept), BF16),
            pltpu.VMEM((NEAR, width, width), F32),
            pltpu.SemaphoreType.DMA((4 + PARTS,)),
        ],
        compiler_params=pltpu.CompilerParams(vmem_limit_bytes=VMEM_LIMIT),
        name="project",
    )(
        sub_size,
        *(
            pltpu.with_memory_space_constraint(x, pltpu.HBM)
            for x in (iface_offset, modes, eigenvalues, row_offset, stiff_coupling)
        ),
    )
    received = [sums[REACH]] + [passed_along(sums[d + REACH], "sub", d) for d in DISTANCES]
    projected, stiff = pl.pallas_call(
        stiffen_kernel,
        in_specs=[in_smem()] + [in_vmem()] * 2,
        out_specs=[in_vmem()] * 2,
        out_shape=[near(blocks, kept, width, dtype=BF16), near(NEAR, width, width)],
        compiler_params=pltpu.CompilerParams(vmem_limit_bytes=VMEM_LIMIT),
        name="stiffen",
    )(iface_offset, eigenvalues, turned)
    factor, *parcels = pl.pallas_call(
        factor_kernel,
        in_specs=[in_vmem()] * (NEAR + 2),
        out_specs=[in_vmem()] * (1 + NEAR),
        out_shape=[array(1, width, width)] + [near(width + ROWS, width)] * NEAR,
        compiler_params=pltpu.CompilerParams(vmem_limit_bytes=VMEM_LIMIT),
        name="factor",
    )(*received, lumped_mass, stiff)
    arrived = [
        parcels[REACH] if d == 0 else passed_along(parcels[REACH - d], "sub", -d)
        for d in range(-REACH, REACH + 1)
    ]
    reduced, coupled = pl.pallas_call(
        transform_kernel,
        in_specs=[in_smem()] + [in_vmem()] * (NEAR + 2),
        out_specs=[in_vmem(), anywhere],
        out_shape=[array(1, width, width), array(blocks, kept, width, dtype=BF16)],
        scratch_shapes=[
            pltpu.VMEM((NEAR, width, 2 * width), BF16),
            pltpu.VMEM((blocks, kept, width), BF16),
            pltpu.SemaphoreType.DMA((blocks // GROUP,)),
        ],
        compiler_params=pltpu.CompilerParams(vmem_limit_bytes=VMEM_LIMIT),
        name="transform",
    )(iface_offset, projected, stiff_iface, *arrived)
    return (reduced, factor, coupled)


def solution(mesh):
    placed = (
        P(("groups", "sub"), None),
        P(("groups", "sub"), None),
        P(("groups", "sub")),
        P(("groups", "sub"), None),
        P(("groups", "sub"), None, None),
        P(("groups", "sub")),
        P(("groups", "sub"), None, None),
        P(("groups", "sub"), None),
    )
    return jax.shard_map(
        per_device,
        mesh=mesh,
        in_specs=placed,
        out_specs=(
            P(("groups", "sub"), None, None),
            P(("groups", "sub"), None, None),
            P(("groups", "sub"), None, None),
        ),
        check_vma=False,
    )
```

time: 66.2 us -> 49.6 us (0.75)
  Pallas kernels: 35.5 us -> 23.6 us
  waiting for transfers between devices: 13.7 us -> 6.3 us
  starting transfers between devices: 14 us -> 16.5 us
    pallas_call x2 -> x3, Pallas kernels: 29.6 us -> 18.8 us  [the longest x1 11.1 us: per_device(): pl.pallas_call(project_kernel, in_specs=[in_smem()] + [pl.BlockSpec(memor...]
    ppermute x12, waiting for transfers between devices: 13.7 us -> 6.3 us  [passed_along(): lax.ppermute(x, axis, [(i, (i + by) % length) for i in range(length)])]
    ppermute x12, starting transfers between devices: 14 us -> 16.5 us  [passed_along(): lax.ppermute(x, axis, [(i, (i + by) % length) for i in range(length)])]
    pallas_call x1, Pallas kernels: 5.93 us -> 4.83 us  [per_device(): pl.pallas_call(factor_kernel, in_specs=[in_vmem()] * (NEAR + 2), out_spec...]
    unnamed x24 -> x8, local copies, waits for them, and re-layouts: 1.22 us -> 1.34 us
  transfers between devices with their start and end apart: 12 -> 12, of which waited for: 7 -> 4; matrix products, arithmetic and copies ran while one was open for 0% -> 0% of each run, Pallas kernels for 0% -> 7%
where the time goes in v2:
time: 49.6 us; the launch traced here: 49.3 us
  Pallas kernels  23.6 us (48%)
  starting transfers between devices  16.5 us (33%)
  waiting for transfers between devices  6.3 us (13%)
  between operations  1.55 us (3%)
  local copies, waits for them, and re-layouts  1.34 us (3%)
    ppermute x12, starting transfers between devices, passed_along(): lax.ppermute(x, axis, [(i, (i + by) % length) for i in range(length)])  16.5 us
    pallas_call x1, Pallas kernels, per_device(): pl.pallas_call(project_kernel, in_specs=[in_smem()] + [pl.BlockSpec(memor...  11.1 us
    ppermute x12, waiting for transfers between devices, passed_along(): lax.ppermute(x, axis, [(i, (i + by) % length) for i in range(length)])  6.3 us
    pallas_call x1, Pallas kernels, per_device(): pl.pallas_call(factor_kernel, in_specs=[in_vmem()] * (NEAR + 2), out_spec...  4.83 us
    pallas_call x1, Pallas kernels, per_device(): pl.pallas_call(transform_kernel, in_specs=[in_smem()] + [in_vmem()] * (NE...  4.5 us
    pallas_call x1, Pallas kernels, per_device(): pl.pallas_call(stiffen_kernel, in_specs=[in_smem()] + [in_vmem()] * 2, ou...  3.23 us
    unnamed x8, local copies, waits for them, and re-layouts  1.34 us
  transfers between devices with their start and end apart: 12, of which 4 were waited for; matrix products, arithmetic and copies ran while one was open for 0% of the time, Pallas kernels for 7%

profile of v2, /device:TPU:1, one launch (start us, length us, event | category | flops | bytes accessed | tf_op | source)
XLA Modules:
  0.0 49.3 jit_solution(4381914041582742342)
XLA Ops:
  0.6 0.0 copy-start.3
  0.6 0.0 copy-start
  1.3 11.1 %project.1 = (bf16[32,128,512]{2,1,0:T(8,128)(2,1)S(1)}, f32[128,128]{1,0:T(8,128)S(1)}, f32[128,128]{1,0:T(8,128)S(1)}, f32[128,128]{1,0:T(8,128)S(1)}, f32[128...) custom-call(s32[1]{0:T(128)S(6)} %copy.11.size, s32[32]{0:T(128)} %offset.5, ...), custom_call_target="tpu_custom_call" | custom-call | tf_op jit(solution)/shard_map/project/pallas_call | solution.py:229
  12.4 5.7 %collective-permute-start = (f32[128,128]{1,0:T(8,128)S(1)}, f32[128,128]{1,0:T(8,128)S(1)}, u32[]{:S(2)}, u32[]{:S(2)}) collective-permute-start(f32[128,128]{1,0:T(8,128)S(1)} %get-tuple-element.26), channel_id=1, source_target_pairs={{0,13},{1,14},{2,15},{3,0},{4,1},{5,2},{6,3},{7,4},{8,5},{9,6},{10... | collective-permute-start | bytes 196616 | tf_op jit(solution)/shard_map/ppermute | solution.py:22
  18.1 0.3 collective-permute-start.1
  18.3 0.2 collective-permute-start.2
  18.5 1.5 %collective-permute-start.3 = (f32[128,128]{1,0:T(8,128)S(1)}, f32[128,128]{1,0:T(8,128)S(1)}, u32[]{:S(2)}, u32[]{:S(2)}) collective-permute-start(f32[128,128]{1,0:T(8,128)S(1)} %get-tuple-element.29), channel_id=1, source_target_pairs={{0,1},{1,2},{2,3},{3,4},{4,5},{5,6},{6,7},{7,8},{8,9},{9,10},{10,1... | collective-permute-start | bytes 196616 | tf_op jit(solution)/shard_map/ppermute | solution.py:22
  20.1 2.1 %collective-permute-start.4 = (f32[128,128]{1,0:T(8,128)S(1)}, f32[128,128]{1,0:T(8,128)S(1)}, u32[]{:S(2)}, u32[]{:S(2)}) collective-permute-start(f32[128,128]{1,0:T(8,128)S(1)} %get-tuple-element.30), channel_id=1, source_target_pairs={{0,2},{1,3},{2,4},{3,5},{4,6},{5,7},{6,8},{7,9},{8,10},{9,11},{10,... | collective-permute-start | bytes 196616 | tf_op jit(solution)/shard_map/ppermute | solution.py:22
  22.2 0.0 collective-permute-done.refs_1_
  22.2 0.0 collective-permute-start.5
  22.2 0.0 copy-start.1
  22.2 0.7 %copy-done.1 = f32[1,512]{1,0:T(1,128)S(1)} copy-done((f32[1,512]{1,0:T(1,128)S(1)}, f32[1,512]{1,0:T(1,128)}, u32[]{:S(2)}) %copy-start.1) | copy-done | bytes 2072
  22.9 0.0 copy-start.2
  22.9 0.7 %copy-done.2 = s32[32]{0:T(128)S(1)} copy-done((s32[32]{0:T(128)S(1)}, s32[32]{0:T(128)}, u32[]{:S(2)}) %copy-start.2) | copy-done | bytes 152
  23.5 3.2 %stiffen.1 = (bf16[32,512,128]{2,1,0:T(8,128)(2,1)S(1)}, f32[7,128,128]{2,1,0:T(8,128)S(1)}) custom-call(s32[32]{0:T(128)S(1)} %copy-done.2, f32[1,512]{1,0:T(1,128)S(1)} %copy-done.1, bf16[32,128,512]{2,1,0:T(8,128)(2,1)S(1)} %get-tuple-element.23.turned), custom_call_target="tpu_custom_call" | custom-call | tf_op jit(solution)/shard_map/stiffen/pallas_call | solution.py:255
  26.8 0.0 collective-permute-done.1.refs_2_
  26.8 0.0 collective-permute-done.2.refs_3_
  26.8 0.0 collective-permute-done.3.refs_4_
  26.8 0.3 collective-permute-done.4.refs_5_
  27.1 1.5 %collective-permute-done.5.refs_6_ = f32[128,128]{1,0:T(8,128)S(1)} collective-permute-done((f32[128,128]{1,0:T(8,128)S(1)}, f32[128,128]{1,0:T(8,128)S(1)}, u32[]{:S(2)}, u32[]{:S(2)}) %collective-permute-start.5) | collective-permute-done | bytes 65568 | tf_op jit(solution)/shard_map/ppermute | solution.py:22
  28.6 0.0 copy-done.3
  28.6 4.8 %factor.1 = (f32[1,128,128]{2,1,0:T(8,128)}, f32[136,128]{1,0:T(8,128)S(1)}, f32[136,128]{1,0:T(8,128)S(1)}, f32[136,128]{1,0:T(8,128)S(1)}, f32[136,128]{1,0:T(...) custom-call(f32[128,128]{1,0:T(8,128)S(1)} %get-tuple-element.25.refs_0_, ...), custom_call_target="tpu_custom_call" | custom-call | tf_op jit(solution)/shard_map/factor/pallas_call | solution.py:263
  33.4 0.0 collective-permute-start.6
  33.4 0.1 collective-permute-start.7
  33.5 0.5 collective-permute-start.8
  34.0 0.4 collective-permute-start.9
  34.4 4.0 %collective-permute-start.10 = (f32[136,128]{1,0:T(8,128)S(1)}, f32[136,128]{1,0:T(8,128)S(1)}, u32[]{:S(2)}, u32[]{:S(2)}) collective-permute-start(f32[136,128]{1,0:T(8,128)S(1)} %get-tuple-element.38), channel_id=1, source_target_pairs={{0,14},{1,15},{2,0},{3,1},{4,2},{5,3},{6,4},{7,5},{8,6},{9,7},{10,... | collective-permute-start | bytes 208904 | tf_op jit(solution)/shard_map/ppermute | solution.py:22
  38.4 2.4 %collective-permute-done.6.refs_0_ = f32[136,128]{1,0:T(8,128)S(1)} collective-permute-done((f32[136,128]{1,0:T(8,128)S(1)}, f32[136,128]{1,0:T(8,128)S(1)}, u32[]{:S(2)}, u32[]{:S(2)}) %collective-permute-start.6) | collective-permute-done | bytes 69664 | tf_op jit(solution)/shard_map/ppermute | solution.py:22
  40.9 1.6 %collective-permute-start.11 = (f32[136,128]{1,0:T(8,128)S(1)}, f32[136,128]{1,0:T(8,128)S(1)}, u32[]{:S(2)}, u32[]{:S(2)}) collective-permute-start(f32[136,128]{1,0:T(8,128)S(1)} %get-tuple-element.39), channel_id=1, source_target_pairs={{0,13},{1,14},{2,15},{3,0},{4,1},{5,2},{6,3},{7,4},{8,5},{9,6},{10... | collective-permute-start | bytes 208904 | tf_op jit(solution)/shard_map/ppermute | solution.py:22
  42.5 0.0 collective-permute-done.7.refs_1_
  42.5 0.0 collective-permute-done.8.refs_2_
  42.5 0.0 collective-permute-done.9.refs_4_
  42.5 0.0 collective-permute-done.10.refs_5_
  42.6 2.1 %collective-permute-done.11.refs_6_ = f32[136,128]{1,0:T(8,128)S(1)} collective-permute-done((f32[136,128]{1,0:T(8,128)S(1)}, f32[136,128]{1,0:T(8,128)S(1)}, u32[]{:S(2)}, u32[]{:S(2)}) %collective-permute-start.11) | collective-permute-done | bytes 69664 | tf_op jit(solution)/shard_map/ppermute | solution.py:22
  44.6 0.0 copy-done
  44.6 4.5 %transform.1 = (f32[1,128,128]{2,1,0:T(8,128)}, bf16[32,512,128]{2,1,0:T(8,128)(2,1)}) custom-call(s32[32]{0:T(128)S(1)} %copy-done.2, bf16[32,512,128]{2,1,0:T(8,128)(2,1)S(1)} %get-tuple-element.24.projected, f32[1,128,128]{2,1,0:T(8,128)S(1)} %copy-done, f32[136,128]{1,0:T(8,128)S(1)} %collective-permute-done.6.refs_0_, ...), custom_call_target="tpu_custom_call" | custom-call | tf_op jit(solution)/shard_map/transform/pallas_call | solution.py:275
Async XLA Ops:
  0.6 27.9 %copy-start.3 = (f32[1,128]{1,0:T(1,128)S(1)}, f32[1,128]{1,0:T(1,128)}, u32[]{:S(2)}) copy-start(f32[1,128]{1,0:T(1,128)} %refs_7_.1) | copy-start | bytes 1540
  0.6 44.0 %copy-start = (f32[1,128,128]{2,1,0:T(8,128)S(1)}, f32[1,128,128]{2,1,0:T(8,128)}, u32[]{:S(2)}) copy-start(f32[1,128,128]{2,1,0:T(8,128)} %stiff_iface.1) | copy-start | bytes 196612
  12.4 9.8 %collective-permute-start = (f32[128,128]{1,0:T(8,128)S(1)}, f32[128,128]{1,0:T(8,128)S(1)}, u32[]{:S(2)}, u32[]{:S(2)}) collective-permute-start(f32[128,128]{1,0:T(8,128)S(1)} %get-tuple-element.26), channel_id=1, source_target_pairs={{0,13},{1,14},{2,15},{3,0},{4,1},{5,2},{6,3},{7,4},{8,5},{9,6},{10... | collective-permute-start | bytes 196616 | tf_op jit(solution)/shard_map/ppermute | solution.py:22
  18.1 8.7 %collective-permute-start.1 = (f32[128,128]{1,0:T(8,128)S(1)}, f32[128,128]{1,0:T(8,128)S(1)}, u32[]{:S(2)}, u32[]{:S(2)}) collective-permute-start(f32[128,128]{1,0:T(8,128)S(1)} %get-tuple-element.27), channel_id=1, source_target_pairs={{0,14},{1,15},{2,0},{3,1},{4,2},{5,3},{6,4},{7,5},{8,6},{9,7},{10,... | collective-permute-start | bytes 196616 | tf_op jit(solution)/shard_map/ppermute | solution.py:22
  18.3 8.5 %collective-permute-start.2 = (f32[128,128]{1,0:T(8,128)S(1)}, f32[128,128]{1,0:T(8,128)S(1)}, u32[]{:S(2)}, u32[]{:S(2)}) collective-permute-start(f32[128,128]{1,0:T(8,128)S(1)} %get-tuple-element.28), channel_id=1, source_target_pairs={{0,15},{1,0},{2,1},{3,2},{4,3},{5,4},{6,5},{7,6},{8,7},{9,8},{10,9... | collective-permute-start | bytes 196616 | tf_op jit(solution)/shard_map/ppermute | solution.py:22
  18.5 8.3 %collective-permute-start.3 = (f32[128,128]{1,0:T(8,128)S(1)}, f32[128,128]{1,0:T(8,128)S(1)}, u32[]{:S(2)}, u32[]{:S(2)}) collective-permute-start(f32[128,128]{1,0:T(8,128)S(1)} %get-tuple-element.29), channel_id=1, source_target_pairs={{0,1},{1,2},{2,3},{3,4},{4,5},{5,6},{6,7},{7,8},{8,9},{9,10},{10,1... | collective-permute-start | bytes 196616 | tf_op jit(solution)/shard_map/ppermute | solution.py:22
  20.1 7.0 %collective-permute-start.4 = (f32[128,128]{1,0:T(8,128)S(1)}, f32[128,128]{1,0:T(8,128)S(1)}, u32[]{:S(2)}, u32[]{:S(2)}) collective-permute-start(f32[128,128]{1,0:T(8,128)S(1)} %get-tuple-element.30), channel_id=1, source_target_pairs={{0,2},{1,3},{2,4},{3,5},{4,6},{5,7},{6,8},{7,9},{8,10},{9,11},{10,... | collective-permute-start | bytes 196616 | tf_op jit(solution)/shard_map/ppermute | solution.py:22
  22.2 6.4 %collective-permute-start.5 = (f32[128,128]{1,0:T(8,128)S(1)}, f32[128,128]{1,0:T(8,128)S(1)}, u32[]{:S(2)}, u32[]{:S(2)}) collective-permute-start(f32[128,128]{1,0:T(8,128)S(1)} %get-tuple-element.31), channel_id=1, source_target_pairs={{0,3},{1,4},{2,5},{3,6},{4,7},{5,8},{6,9},{7,10},{8,11},{9,12},{10... | collective-permute-start | bytes 196616 | tf_op jit(solution)/shard_map/ppermute | solution.py:22
  22.2 0.7 %copy-start.1 = (f32[1,512]{1,0:T(1,128)S(1)}, f32[1,512]{1,0:T(1,128)}, u32[]{:S(2)}) copy-start(f32[1,512]{1,0:T(1,128)} %eigen.3) | copy-start | bytes 6148
  22.9 0.7 %copy-start.2 = (s32[32]{0:T(128)S(1)}, s32[32]{0:T(128)}, u32[]{:S(2)}) copy-start(s32[32]{0:T(128)} %offset.5) | copy-start | bytes 388
  33.4 7.5 %collective-permute-start.6 = (f32[136,128]{1,0:T(8,128)S(1)}, f32[136,128]{1,0:T(8,128)S(1)}, u32[]{:S(2)}, u32[]{:S(2)}) collective-permute-start(f32[136,128]{1,0:T(8,128)S(1)} %get-tuple-element.33), channel_id=1, source_target_pairs={{0,3},{1,4},{2,5},{3,6},{4,7},{5,8},{6,9},{7,10},{8,11},{9,12},{10... | collective-permute-start | bytes 208904 | tf_op jit(solution)/shard_map/ppermute | solution.py:22
  33.4 9.1 %collective-permute-start.7 = (f32[136,128]{1,0:T(8,128)S(1)}, f32[136,128]{1,0:T(8,128)S(1)}, u32[]{:S(2)}, u32[]{:S(2)}) collective-permute-start(f32[136,128]{1,0:T(8,128)S(1)} %get-tuple-element.34), channel_id=1, source_target_pairs={{0,2},{1,3},{2,4},{3,5},{4,6},{5,7},{6,8},{7,9},{8,10},{9,11},{10,... | collective-permute-start | bytes 208904 | tf_op jit(solution)/shard_map/ppermute | solution.py:22
  33.5 9.0 %collective-permute-start.8 = (f32[136,128]{1,0:T(8,128)S(1)}, f32[136,128]{1,0:T(8,128)S(1)}, u32[]{:S(2)}, u32[]{:S(2)}) collective-permute-start(f32[136,128]{1,0:T(8,128)S(1)} %get-tuple-element.35), channel_id=1, source_target_pairs={{0,1},{1,2},{2,3},{3,4},{4,5},{5,6},{6,7},{7,8},{8,9},{9,10},{10,1... | collective-permute-start | bytes 208904 | tf_op jit(solution)/shard_map/ppermute | solution.py:22
  34.0 8.5 %collective-permute-start.9 = (f32[136,128]{1,0:T(8,128)S(1)}, f32[136,128]{1,0:T(8,128)S(1)}, u32[]{:S(2)}, u32[]{:S(2)}) collective-permute-start(f32[136,128]{1,0:T(8,128)S(1)} %get-tuple-element.37), channel_id=1, source_target_pairs={{0,15},{1,0},{2,1},{3,2},{4,3},{5,4},{6,5},{7,6},{8,7},{9,8},{10,9... | collective-permute-start | bytes 208904 | tf_op jit(solution)/shard_map/ppermute | solution.py:22
  34.4 8.2 %collective-permute-start.10 = (f32[136,128]{1,0:T(8,128)S(1)}, f32[136,128]{1,0:T(8,128)S(1)}, u32[]{:S(2)}, u32[]{:S(2)}) collective-permute-start(f32[136,128]{1,0:T(8,128)S(1)} %get-tuple-element.38), channel_id=1, source_target_pairs={{0,14},{1,15},{2,0},{3,1},{4,2},{5,3},{6,4},{7,5},{8,6},{9,7},{10,... | collective-permute-start | bytes 208904 | tf_op jit(solution)/shard_map/ppermute | solution.py:22
  40.9 3.7 %collective-permute-start.11 = (f32[136,128]{1,0:T(8,128)S(1)}, f32[136,128]{1,0:T(8,128)S(1)}, u32[]{:S(2)}, u32[]{:S(2)}) collective-permute-start(f32[136,128]{1,0:T(8,128)S(1)} %get-tuple-element.39), channel_id=1, source_target_pairs={{0,13},{1,14},{2,15},{3,0},{4,1},{5,2},{6,3},{7,4},{8,5},{9,6},{10... | collective-permute-start | bytes 208904 | tf_op jit(solution)/shard_map/ppermute | solution.py:22

commit v3 on v2

--- a/solution.py
+++ b/solution.py
@@ -14,13 +14,44 @@
 VMEM_LIMIT = 24 << 20
 F32 = jnp.float32
 BF16 = jnp.bfloat16
-DISTANCES = tuple(d for d in range(-REACH, REACH + 1) if d != 0)
-
-
-def passed_along(x, axis, by):
-    length = lax.axis_size(axis)
-    moved = lax.ppermute(x, axis, [(i, (i + by) % length) for i in range(length)])
-    return pltpu.with_memory_space_constraint(moved, pltpu.VMEM)
+
+
+def exchanges(length):
+    group = REACH + 1
+    if length % group or length < 2 * group:
+        return [
+            ([(i, (i + d) % length) for i in range(length)], [d] * group)
+            for d in range(-REACH, REACH + 1)
+            if d != 0
+        ]
+    plans = []
+    for crossing in (((3, 0), (2, 1)), ((1, 0), (3, 2)), ((2, 0), (3, 1))):
+        far = [0] * group
+        for high, low in crossing:
+            far[high] = group + low - high
+            far[low] = high - low - group
+        plans.append(far)
+    for mask in range(1, group):
+        plans.append([(k ^ mask) - k for k in range(group)])
+    plans = [plans[k] for k in (2, 1, 0, 3, 4, 5)]
+    return [
+        ([(i, (i + far[i % group]) % length) for i in range(length)], far) for far in plans
+    ]
+
+
+def slots():
+    place = lax.rem(lax.axis_index("sub"), REACH + 1)
+    found = []
+    for _, far in exchanges(lax.axis_size("sub")):
+        slot = jnp.int32(far[0] + REACH)
+        for k in range(1, REACH + 1):
+            slot = jnp.where(place == k, far[k] + REACH, slot)
+        found.append(slot)
+    return found
+
+
+def exchanged(x, pairs):
+    return pltpu.with_memory_space_constraint(lax.ppermute(x, "sub", pairs), pltpu.VMEM)
 
 
 def halves(x):
@@ -41,9 +72,46 @@
     )
 
 
-def project_kernel(size, offset, modes, eigen, row_offset, coupling, turned, *rest):
+def pack(full):
+    width = full.shape[1]
+    half = width // 2
+    row, column = iotas((half, width))
+    low = full[half:]
+    from_low = (column < half) | (column - half > row)
+    diagonal = jnp.sum(jnp.where(column - half == row, low, 0.0), axis=0, keepdims=True)
+    return (
+        jnp.where(from_low, low, pltpu.roll(full[:half], half, 1)),
+        jnp.broadcast_to(diagonal, (ROWS, width)),
+    )
+
+
+def unpack(packed, extra):
+    half, width = packed.shape[0] - ROWS, packed.shape[1]
+    row, column = iotas((half, width))
+    low = packed[:half]
+    top = pltpu.roll(low, half, 1)
+    off = jnp.concatenate(
+        [
+            jnp.where((column < half) & (row > column), top, 0.0),
+            jnp.where((column < half) | (column - half > row), low, 0.0),
+        ],
+        axis=0,
+    )
+    diagonal = jnp.concatenate(
+        [
+            jnp.where(row == column, top + extra, 0.0),
+            jnp.where(column - half == row, packed[half : half + 1] + extra, 0.0),
+        ],
+        axis=0,
+    )
+    return off + off.T + diagonal
+
+
+def project_kernel(
+    size, offset, modes, eigen, row_offset, coupling, turned, offsets, inverse, *rest
+):
     packed = rest[:NEAR]
-    offsets, rows, values, wants, blocks_in, span_rows, picked, sums, arrived = rest[NEAR:]
+    rows, values, wants, blocks_in, span_rows, picked, sums, arrived = rest[NEAR:]
     blocks, picks, width = coupling.shape
     span = span_rows.shape[0]
     part = rows.shape[0] // PARTS
@@ -64,8 +132,8 @@
     for copy in copies[:3]:
         copy.wait()
     wanted = (span - 1 - wants[...]).T
-    inverse = 1.0 / values[...]
-    weight = inverse * inverse
+    inverse[...] = 1.0 / values[...]
+    weight = inverse[...] * inverse[...]
     start = size[0] - span
     base = jnp.minimum(start // TILE * TILE, rows.shape[0] - span - TILE)
     for copy in copies[3:]:
@@ -92,14 +160,15 @@
                 for b in range(i * GROUP, (i + 1) * GROUP)
             ]
             picked[i % 2] = dot(jnp.concatenate(chosen, axis=0), span_rows[...]).astype(BF16)
-    for k in range(NEAR):
-        packed[k][...] = sums[k]
-
-
-def stiffen_kernel(offset, eigen, turned, projected, sums):
+    half = width // 2
+    for message, slot in zip(packed, slots() + [REACH], strict=True):
+        message[:half, :], message[half:, :] = pack(sums[slot])
+
+
+def stiffen_kernel(offset, inverse, turned, projected, sums):
     width = sums.shape[1]
     sums[...] = jnp.zeros_like(sums)
-    weight = 1.0 / eigen[...]
+    weight = inverse[...]
     for b in range(turned.shape[0]):
         block = turned[b]
         stiff = halves(block.astype(F32) * weight)
@@ -117,17 +186,17 @@
     for piece in received[1:]:
         total = total + piece[...]
     row, column = iotas((width, width))
-    lower = jnp.where(row > column, total, 0.0)
-    mass = lower + lower.T + jnp.where(row == column, total + lumped[...], 0.0)
-    identity = jnp.where(row == column, 1.0, 0.0)
+    mass = unpack(total, lumped[...])
     panels = width // ROWS
-    left = [mass[p * ROWS : (p + 1) * ROWS] for p in range(panels)]
-    right = [identity[p * ROWS : (p + 1) * ROWS] for p in range(panels)]
+    work = [mass[p * ROWS : (p + 1) * ROWS] for p in range(panels)]
     spread = (ROWS, width)
+    line, lane = iotas(spread)
+    corners = []
     for p in range(panels):
         at = p * ROWS
+        inside = (lane >= at) & (lane < at + ROWS)
         columns = [
-            jnp.broadcast_to(left[p][:, at + j : at + j + 1], spread) for j in range(ROWS)
+            jnp.broadcast_to(work[p][:, at + j : at + j + 1], spread) for j in range(ROWS)
         ]
         pivot = {
             (i, j): jnp.broadcast_to(columns[j][i : i + 1, :], spread)
@@ -135,44 +204,58 @@
             for i in range(j, ROWS)
         }
         scale = []
+        for j in range(0, ROWS, 2):
+            first, cross = pivot[j, j], pivot[j + 1, j]
+            determinant = first * pivot[j + 1, j + 1] - cross * cross
+            root, both = lax.rsqrt(first), lax.rsqrt(determinant)
+            scale += [root, both * (first * root)]
+            pivot[j + 1, j] = cross * root
+            shared = both * root
+            for i in range(j + 2, ROWS):
+                ahead = first * pivot[i, j + 1] - cross * pivot[i, j]
+                pivot[i, j] = pivot[i, j] * root
+                pivot[i, j + 1] = ahead * shared
+            for k in range(j + 2, ROWS):
+                for i in range(k, ROWS):
+                    pivot[i, k] = (pivot[i, k] - pivot[i, j] * pivot[k, j]) - pivot[
+                        i, j + 1
+                    ] * pivot[k, j + 1]
+        top = jnp.where(inside, jnp.where(lane - at == line, 1.0, 0.0), work[p])
+        solved = []
         for j in range(ROWS):
-            scale.append(lax.rsqrt(pivot[j, j]))
-            for i in range(j + 1, ROWS):
-                pivot[i, j] = pivot[i, j] * scale[j]
-            for k in range(j + 1, ROWS):
-                for i in range(k, ROWS):
-                    pivot[i, k] = pivot[i, k] - pivot[i, j] * pivot[k, j]
-        solved_left, solved_right = [], []
-        for j in range(ROWS):
-            a = jnp.broadcast_to(left[p][j : j + 1, :], spread)
-            x = jnp.broadcast_to(right[p][j : j + 1, :], spread)
+            a = jnp.broadcast_to(top[j : j + 1, :], spread)
             for k in range(j):
-                a = a - pivot[j, k] * solved_left[k]
-                x = x - pivot[j, k] * solved_right[k]
-            solved_left.append(a * scale[j])
-            solved_right.append(x * scale[j])
-        for q in range(p + 1, panels):
+                a = a - pivot[j, k] * solved[k]
+            solved.append(a * scale[j])
+        for q in range(p, panels):
             below = []
             for j in range(ROWS):
-                v = jnp.broadcast_to(left[q][:, at + j : at + j + 1], spread)
+                v = jnp.broadcast_to(work[q][:, at + j : at + j + 1], spread)
                 for k in range(j):
                     v = v - pivot[j, k] * below[k]
                 below.append(v * scale[j])
-            for j in range(ROWS):
-                left[q] = left[q] - below[j] * solved_left[j]
-                right[q] = right[q] - below[j] * solved_right[j]
-        line, _ = iotas(spread)
-        kept_left, kept_right = solved_left[0], solved_right[0]
+            if q == p:
+                corner = jnp.zeros(spread, F32)
+                for j in range(ROWS):
+                    corner = jnp.where((lane == at + j) & (line >= j), below[j], corner)
+                corners.append(corner)
+            else:
+                left = jnp.where(inside, 0.0, work[q])
+                for j in range(ROWS):
+                    left = left - below[j] * solved[j]
+                work[q] = left
+        kept = solved[0]
         for j in range(1, ROWS):
-            kept_left = jnp.where(line == j, solved_left[j], kept_left)
-            kept_right = jnp.where(line == j, solved_right[j], kept_right)
-        left[p], right[p] = kept_left, kept_right
-    inverse = jnp.concatenate(right, axis=0)
-    for k in range(NEAR):
-        parcels[k][0:width, :] = jnp.where(row >= column, inverse, stiff[k])
-        diagonal = jnp.sum(jnp.where(row == column, stiff[k], 0.0), axis=0, keepdims=True)
-        parcels[k][width:, :] = jnp.broadcast_to(diagonal, (ROWS, width))
-    factor[0] = jnp.where(row <= column, jnp.concatenate(left, axis=0), 0.0).T
+            kept = jnp.where(line == j, solved[j], kept)
+        work[p] = kept
+    inverse = jnp.concatenate(work, axis=0)
+    for parcel, slot in zip(parcels, slots() + [REACH], strict=True):
+        mine = stiff[slot]
+        parcel[0:width, :] = jnp.where(row >= column, inverse, mine)
+        diagonal = jnp.sum(jnp.where(row == column, mine, 0.0), axis=0, keepdims=True)
+        parcel[width:, :] = jnp.broadcast_to(diagonal, (ROWS, width))
+    outer = jnp.where(row // ROWS < column // ROWS, inverse, 0.0)
+    factor[0] = outer.T + jnp.concatenate(corners, axis=0)
 
 
 def transform_kernel(offset, projected, stiff_iface, *refs):
@@ -182,13 +265,13 @@
     row, column = iotas((width, width))
     upper = jnp.zeros((width, width), F32)
     diagonal = jnp.zeros((1, width), F32)
-    for k in range(NEAR):
-        piece = parcels[k][0:width, :]
+    for parcel, slot in zip(parcels, slots() + [REACH], strict=True):
+        piece = parcel[0:width, :]
         high, low = halves(jnp.where(row >= column, piece, 0.0))
-        split[k, :, 0:width] = high
-        split[k, :, width:] = low
+        split[slot, :, 0:width] = high
+        split[slot, :, width:] = low
         upper = upper + jnp.where(row < column, piece, 0.0)
-        diagonal = diagonal + parcels[k][width : width + 1, :]
+        diagonal = diagonal + parcel[width : width + 1, :]
     copies = []
     for first in range(0, blocks, GROUP):
         for b in range(first, first + GROUP):
@@ -226,13 +309,17 @@
         return pltpu.VMEM(shape, dtype)
 
     anywhere = pl.BlockSpec(memory_space=pl.ANY)
-    turned, *sums = pl.pallas_call(
+    turned, offsets, inverse, *sums = pl.pallas_call(
         project_kernel,
         in_specs=[in_smem()] + [pl.BlockSpec(memory_space=pltpu.HBM)] * 5,
-        out_specs=[in_vmem()] * (1 + NEAR),
-        out_shape=[near(blocks, width, kept, dtype=BF16)] + [near(width, width)] * NEAR,
+        out_specs=[in_vmem(), in_smem(), in_vmem()] + [in_vmem()] * NEAR,
+        out_shape=[
+            near(blocks, width, kept, dtype=BF16),
+            pltpu.SMEM((blocks,), jnp.int32),
+            near(1, kept),
+        ]
+        + [near(width // 2 + ROWS, width)] * NEAR,
         scratch_shapes=[
-            pltpu.SMEM(iface_offset.shape, jnp.int32),
             pltpu.VMEM(modes.shape, BF16),
             pltpu.VMEM(eigenvalues.shape, F32),
             pltpu.VMEM(row_offset.shape, jnp.int32),
@@ -251,7 +338,8 @@
             for x in (iface_offset, modes, eigenvalues, row_offset, stiff_coupling)
         ),
     )
-    received = [sums[REACH]] + [passed_along(sums[d + REACH], "sub", d) for d in DISTANCES]
+    plans = [pairs for pairs, _ in exchanges(lax.axis_size("sub"))]
+    received = [exchanged(x, pairs) for x, pairs in zip(sums, plans)] + sums[-1:]
     projected, stiff = pl.pallas_call(
         stiffen_kernel,
         in_specs=[in_smem()] + [in_vmem()] * 2,
@@ -259,7 +347,7 @@
         out_shape=[near(blocks, kept, width, dtype=BF16), near(NEAR, width, width)],
         compiler_params=pltpu.CompilerParams(vmem_limit_bytes=VMEM_LIMIT),
         name="stiffen",
-    )(iface_offset, eigenvalues, turned)
+    )(offsets, inverse, turned)
     factor, *parcels = pl.pallas_call(
         factor_kernel,
         in_specs=[in_vmem()] * (NEAR + 2),
@@ -268,10 +356,7 @@
         compiler_params=pltpu.CompilerParams(vmem_limit_bytes=VMEM_LIMIT),
         name="factor",
     )(*received, lumped_mass, stiff)
-    arrived = [
-        parcels[REACH] if d == 0 else passed_along(parcels[REACH - d], "sub", -d)
-        for d in range(-REACH, REACH + 1)
-    ]
+    arrived = [exchanged(x, pairs) for x, pairs in zip(parcels, plans)] + parcels[-1:]
     reduced, coupled = pl.pallas_call(
         transform_kernel,
         in_specs=[in_smem()] + [in_vmem()] * (NEAR + 2),
@@ -284,7 +369,7 @@
         ],
         compiler_params=pltpu.CompilerParams(vmem_limit_bytes=VMEM_LIMIT),
         name="transform",
-    )(iface_offset, projected, stiff_iface, *arrived)
+    )(offsets, projected, stiff_iface, *arrived)
     return (reduced, factor, coupled)
 
 

time: 49.6 us -> 46.5 us (0.938)
  Pallas kernels: 23.6 us -> 22.2 us
  local copies, waits for them, and re-layouts: 1.34 us -> 0.01 us
    unnamed x8 -> x4, local copies, waits for them, and re-layouts: 1.34 us -> 0.01 us
    pallas_call x1, Pallas kernels: 4.5 us -> 3.95 us  [per_device(): pl.pallas_call(transform_kernel, in_specs=[in_smem()] + [in_vmem()] * (NE...]
  transfers between devices with their start and end apart: 12 -> 12, of which waited for: 4 -> 5; matrix products, arithmetic and copies ran while one was open for 0% -> 0% of each run, Pallas kernels for 7% -> 6%
where the time goes in v3:
time: 46.5 us; the launch traced here: 46 us
  Pallas kernels  22.2 us (48%)
  starting transfers between devices  16.3 us (35%)
  waiting for transfers between devices  5.87 us (13%)
  between operations  1.55 us (3%)
    ppermute x12, starting transfers between devices, exchanged(): lax.ppermute(x, 'sub', pairs)  16.3 us
    pallas_call x1, Pallas kernels, per_device(): pl.pallas_call(project_kernel, in_specs=[in_smem()] + [pl.BlockSpec(memor...  11.1 us
    ppermute x12, waiting for transfers between devices, exchanged(): lax.ppermute(x, 'sub', pairs)  5.87 us
    pallas_call x1, Pallas kernels, per_device(): pl.pallas_call(factor_kernel, in_specs=[in_vmem()] * (NEAR + 2), out_spec...  4.35 us
    pallas_call x1, Pallas kernels, per_device(): pl.pallas_call(transform_kernel, in_specs=[in_smem()] + [in_vmem()] * (NE...  3.95 us
    pallas_call x1, Pallas kernels, per_device(): pl.pallas_call(stiffen_kernel, in_specs=[in_smem()] + [in_vmem()] * 2, ou...  2.83 us
  transfers between devices with their start and end apart: 12, of which 5 were waited for; matrix products, arithmetic and copies ran while one was open for 0% of the time, Pallas kernels for 6%

profile of v3, /device:TPU:1, one launch (start us, length us, event | category | flops | bytes accessed | tf_op | source)
XLA Modules:
  0.0 46.0 jit_solution(16627216448582013366)
XLA Ops:
  0.6 0.0 copy-start.1
  0.6 0.0 copy-start
  1.3 11.1 %project.1 = (bf16[32,128,512]{2,1,0:T(8,128)(2,1)S(1)}, s32[32]{0:T(128)S(4)}, f32[1,512]{1,0:T(1,128)S(1)}, f32[72,128]{1,0:T(8,128)S(1)}, f32[72,128]{1,0:T(8...) custom-call(s32[1]{0:T(128)S(6)} %copy.11.size, ...), custom_call_target="tpu_custom_call" | custom-call | tf_op jit(solution)/shard_map/project/pallas_call | solution.py:312
  12.4 5.1 %collective-permute-start = (f32[72,128]{1,0:T(8,128)S(1)}, f32[72,128]{1,0:T(8,128)S(1)}, u32[]{:S(2)}, u32[]{:S(2)}) collective-permute-start(f32[72,128]{1,0:T(8,128)S(1)} %get-tuple-element.29), channel_id=1, source_target_pairs={{0,14},{1,15},{2,4},{3,5},{4,2},{5,3},{6,8},{7,9},{8,6},{9,7},{10,... | collective-permute-start | bytes 110600 | tf_op jit(solution)/shard_map/ppermute | solution.py:54
  17.6 0.0 collective-permute-start.1
  17.6 1.7 %collective-permute-start.2 = (f32[72,128]{1,0:T(8,128)S(1)}, f32[72,128]{1,0:T(8,128)S(1)}, u32[]{:S(2)}, u32[]{:S(2)}) collective-permute-start(f32[72,128]{1,0:T(8,128)S(1)} %get-tuple-element.31), channel_id=1, source_target_pairs={{0,15},{1,14},{2,5},{3,4},{4,3},{5,2},{6,9},{7,8},{8,7},{9,6},{10,... | collective-permute-start | bytes 110600 | tf_op jit(solution)/shard_map/ppermute | solution.py:54
  19.3 0.7 %collective-permute-start.3 = (f32[72,128]{1,0:T(8,128)S(1)}, f32[72,128]{1,0:T(8,128)S(1)}, u32[]{:S(2)}, u32[]{:S(2)}) collective-permute-start(f32[72,128]{1,0:T(8,128)S(1)} %get-tuple-element.32), channel_id=1, source_target_pairs={{0,1},{1,0},{2,3},{3,2},{4,5},{5,4},{6,7},{7,6},{8,9},{9,8},{10,11... | collective-permute-start | bytes 110600 | tf_op jit(solution)/shard_map/ppermute | solution.py:54
  20.0 0.5 %collective-permute-start.4 = (f32[72,128]{1,0:T(8,128)S(1)}, f32[72,128]{1,0:T(8,128)S(1)}, u32[]{:S(2)}, u32[]{:S(2)}) collective-permute-start(f32[72,128]{1,0:T(8,128)S(1)} %get-tuple-element.33), channel_id=1, source_target_pairs={{0,2},{1,3},{2,0},{3,1},{4,6},{5,7},{6,4},{7,5},{8,10},{9,11},{10,... | collective-permute-start | bytes 110600 | tf_op jit(solution)/shard_map/ppermute | solution.py:54
  20.5 0.0 collective-permute-done.refs_0_
  20.5 1.1 %collective-permute-start.5 = (f32[72,128]{1,0:T(8,128)S(1)}, f32[72,128]{1,0:T(8,128)S(1)}, u32[]{:S(2)}, u32[]{:S(2)}) collective-permute-start(f32[72,128]{1,0:T(8,128)S(1)} %get-tuple-element.34), channel_id=1, source_target_pairs={{0,3},{1,2},{2,1},{3,0},{4,7},{5,6},{6,5},{7,4},{8,11},{9,10},{10,... | collective-permute-start | bytes 110600 | tf_op jit(solution)/shard_map/ppermute | solution.py:54
  21.6 2.8 %stiffen.1 = (bf16[32,512,128]{2,1,0:T(8,128)(2,1)S(1)}, f32[7,128,128]{2,1,0:T(8,128)S(1)}) custom-call(s32[32]{0:T(128)S(4)} %get-tuple-element.25.offset, f32[1,512]{1,0:T(1,128)S(1)} %get-tuple-element.26.inverse, bf16[32,128,512]{2,1,0:T(8,128)(2,1)S(1)} %get-tuple-element.27.turned), custom_call_target="tpu_custom_call" | custom-call | tf_op jit(solution)/shard_map/stiffen/pallas_call | solution.py:343
  24.5 0.0 collective-permute-done.1.refs_1_
  24.5 0.0 collective-permute-done.2.refs_2_
  24.5 0.0 collective-permute-done.3.refs_3_
  24.5 0.0 collective-permute-done.4.refs_4_
  24.5 0.6 %collective-permute-done.5.refs_5_ = f32[72,128]{1,0:T(8,128)S(1)} collective-permute-done((f32[72,128]{1,0:T(8,128)S(1)}, f32[72,128]{1,0:T(8,128)S(1)}, u32[]{:S(2)}, u32[]{:S(2)}) %collective-permute-start.5) | collective-permute-done | bytes 36896 | tf_op jit(solution)/shard_map/ppermute | solution.py:54
  25.1 0.0 copy-done.1
  25.2 4.4 %factor.1 = (f32[1,128,128]{2,1,0:T(8,128)}, f32[136,128]{1,0:T(8,128)S(1)}, f32[136,128]{1,0:T(8,128)S(1)}, f32[136,128]{1,0:T(8,128)S(1)}, f32[136,128]{1,0:T(...) custom-call(f32[72,128]{1,0:T(8,128)S(1)} %collective-permute-done.refs_0_, ...), custom_call_target="tpu_custom_call" | custom-call | tf_op jit(solution)/shard_map/factor/pallas_call | solution.py:351
  29.5 2.5 %collective-permute-start.6 = (f32[136,128]{1,0:T(8,128)S(1)}, f32[136,128]{1,0:T(8,128)S(1)}, u32[]{:S(2)}, u32[]{:S(2)}) collective-permute-start(f32[136,128]{1,0:T(8,128)S(1)} %get-tuple-element.37), channel_id=1, source_target_pairs={{0,14},{1,15},{2,4},{3,5},{4,2},{5,3},{6,8},{7,9},{8,6},{9,7},{10,... | collective-permute-start | bytes 208904 | tf_op jit(solution)/shard_map/ppermute | solution.py:54
  32.0 0.0 collective-permute-start.7
  32.0 3.0 %collective-permute-start.8 = (f32[136,128]{1,0:T(8,128)S(1)}, f32[136,128]{1,0:T(8,128)S(1)}, u32[]{:S(2)}, u32[]{:S(2)}) collective-permute-start(f32[136,128]{1,0:T(8,128)S(1)} %get-tuple-element.39), channel_id=1, source_target_pairs={{0,15},{1,14},{2,5},{3,4},{4,3},{5,2},{6,9},{7,8},{8,7},{9,6},{10,... | collective-permute-start | bytes 208904 | tf_op jit(solution)/shard_map/ppermute | solution.py:54
  35.0 0.0 collective-permute-start.9
  35.0 0.0 collective-permute-start.10
  35.0 0.5 %collective-permute-done.6.refs_0_ = f32[136,128]{1,0:T(8,128)S(1)} collective-permute-done((f32[136,128]{1,0:T(8,128)S(1)}, f32[136,128]{1,0:T(8,128)S(1)}, u32[]{:S(2)}, u32[]{:S(2)}) %collective-permute-start.6) | collective-permute-done | bytes 69664 | tf_op jit(solution)/shard_map/ppermute | solution.py:54
  35.5 1.6 %collective-permute-start.11 = (f32[136,128]{1,0:T(8,128)S(1)}, f32[136,128]{1,0:T(8,128)S(1)}, u32[]{:S(2)}, u32[]{:S(2)}) collective-permute-start(f32[136,128]{1,0:T(8,128)S(1)} %get-tuple-element.42), channel_id=1, source_target_pairs={{0,3},{1,2},{2,1},{3,0},{4,7},{5,6},{6,5},{7,4},{8,11},{9,10},{10,... | collective-permute-start | bytes 208904 | tf_op jit(solution)/shard_map/ppermute | solution.py:54
  37.1 0.0 collective-permute-done.7.refs_1_
  37.1 1.4 %collective-permute-done.8.refs_2_ = f32[136,128]{1,0:T(8,128)S(1)} collective-permute-done((f32[136,128]{1,0:T(8,128)S(1)}, f32[136,128]{1,0:T(8,128)S(1)}, u32[]{:S(2)}, u32[]{:S(2)}) %collective-permute-start.8) | collective-permute-done | bytes 69664 | tf_op jit(solution)/shard_map/ppermute | solution.py:54
  38.5 0.0 collective-permute-done.9.refs_3_
  38.5 1.8 %collective-permute-done.10.refs_4_ = f32[136,128]{1,0:T(8,128)S(1)} collective-permute-done((f32[136,128]{1,0:T(8,128)S(1)}, f32[136,128]{1,0:T(8,128)S(1)}, u32[]{:S(2)}, u32[]{:S(2)}) %collective-permute-start.10) | collective-permute-done | bytes 69664 | tf_op jit(solution)/shard_map/ppermute | solution.py:54
  40.3 1.6 %collective-permute-done.11.refs_5_ = f32[136,128]{1,0:T(8,128)S(1)} collective-permute-done((f32[136,128]{1,0:T(8,128)S(1)}, f32[136,128]{1,0:T(8,128)S(1)}, u32[]{:S(2)}, u32[]{:S(2)}) %collective-permute-start.11) | collective-permute-done | bytes 69664 | tf_op jit(solution)/shard_map/ppermute | solution.py:54
  41.9 0.0 copy-done
  41.9 4.0 %transform.1 = (f32[1,128,128]{2,1,0:T(8,128)}, bf16[32,512,128]{2,1,0:T(8,128)(2,1)}) custom-call(s32[32]{0:T(128)S(4)} %get-tuple-element.25.offset, bf16[32,512,128]{2,1,0:T(8,128)(2,1)S(1)} %get-tuple-element.28.projected, f32[1,128,128]{2,1,0:T(8,128)S(1)} %copy-done, f32[136,128]{1,0:T(8,128)S(1)} %collective-permute-done.6.refs_0_, ...), custom_call_target="tpu_custom_call" | custom-call | tf_op jit(solution)/shard_map/transform/pallas_call | solution.py:360
Async XLA Ops:
  0.6 24.5 %copy-start.1 = (f32[1,128]{1,0:T(1,128)S(1)}, f32[1,128]{1,0:T(1,128)}, u32[]{:S(2)}) copy-start(f32[1,128]{1,0:T(1,128)} %refs_7_.1) | copy-start | bytes 1540
  0.6 41.2 %copy-start = (f32[1,128,128]{2,1,0:T(8,128)S(1)}, f32[1,128,128]{2,1,0:T(8,128)}, u32[]{:S(2)}) copy-start(f32[1,128,128]{2,1,0:T(8,128)} %stiff_iface.1) | copy-start | bytes 196612
  12.4 8.1 %collective-permute-start = (f32[72,128]{1,0:T(8,128)S(1)}, f32[72,128]{1,0:T(8,128)S(1)}, u32[]{:S(2)}, u32[]{:S(2)}) collective-permute-start(f32[72,128]{1,0:T(8,128)S(1)} %get-tuple-element.29), channel_id=1, source_target_pairs={{0,14},{1,15},{2,4},{3,5},{4,2},{5,3},{6,8},{7,9},{8,6},{9,7},{10,... | collective-permute-start | bytes 110600 | tf_op jit(solution)/shard_map/ppermute | solution.py:54
  17.6 6.9 %collective-permute-start.1 = (f32[72,128]{1,0:T(8,128)S(1)}, f32[72,128]{1,0:T(8,128)S(1)}, u32[]{:S(2)}, u32[]{:S(2)}) collective-permute-start(f32[72,128]{1,0:T(8,128)S(1)} %get-tuple-element.30), channel_id=1, source_target_pairs={{0,13},{1,4},{2,15},{3,6},{4,1},{5,8},{6,3},{7,10},{8,5},{9,12},{1... | collective-permute-start | bytes 110600 | tf_op jit(solution)/shard_map/ppermute | solution.py:54
  17.6 6.9 %collective-permute-start.2 = (f32[72,128]{1,0:T(8,128)S(1)}, f32[72,128]{1,0:T(8,128)S(1)}, u32[]{:S(2)}, u32[]{:S(2)}) collective-permute-start(f32[72,128]{1,0:T(8,128)S(1)} %get-tuple-element.31), channel_id=1, source_target_pairs={{0,15},{1,14},{2,5},{3,4},{4,3},{5,2},{6,9},{7,8},{8,7},{9,6},{10,... | collective-permute-start | bytes 110600 | tf_op jit(solution)/shard_map/ppermute | solution.py:54
  19.3 5.2 %collective-permute-start.3 = (f32[72,128]{1,0:T(8,128)S(1)}, f32[72,128]{1,0:T(8,128)S(1)}, u32[]{:S(2)}, u32[]{:S(2)}) collective-permute-start(f32[72,128]{1,0:T(8,128)S(1)} %get-tuple-element.32), channel_id=1, source_target_pairs={{0,1},{1,0},{2,3},{3,2},{4,5},{5,4},{6,7},{7,6},{8,9},{9,8},{10,11... | collective-permute-start | bytes 110600 | tf_op jit(solution)/shard_map/ppermute | solution.py:54
  20.0 4.5 %collective-permute-start.4 = (f32[72,128]{1,0:T(8,128)S(1)}, f32[72,128]{1,0:T(8,128)S(1)}, u32[]{:S(2)}, u32[]{:S(2)}) collective-permute-start(f32[72,128]{1,0:T(8,128)S(1)} %get-tuple-element.33), channel_id=1, source_target_pairs={{0,2},{1,3},{2,0},{3,1},{4,6},{5,7},{6,4},{7,5},{8,10},{9,11},{10,... | collective-permute-start | bytes 110600 | tf_op jit(solution)/shard_map/ppermute | solution.py:54
  20.5 4.7 %collective-permute-start.5 = (f32[72,128]{1,0:T(8,128)S(1)}, f32[72,128]{1,0:T(8,128)S(1)}, u32[]{:S(2)}, u32[]{:S(2)}) collective-permute-start(f32[72,128]{1,0:T(8,128)S(1)} %get-tuple-element.34), channel_id=1, source_target_pairs={{0,3},{1,2},{2,1},{3,0},{4,7},{5,6},{6,5},{7,4},{8,11},{9,10},{10,... | collective-permute-start | bytes 110600 | tf_op jit(solution)/shard_map/ppermute | solution.py:54
  29.5 6.0 %collective-permute-start.6 = (f32[136,128]{1,0:T(8,128)S(1)}, f32[136,128]{1,0:T(8,128)S(1)}, u32[]{:S(2)}, u32[]{:S(2)}) collective-permute-start(f32[136,128]{1,0:T(8,128)S(1)} %get-tuple-element.37), channel_id=1, source_target_pairs={{0,14},{1,15},{2,4},{3,5},{4,2},{5,3},{6,8},{7,9},{8,6},{9,7},{10,... | collective-permute-start | bytes 208904 | tf_op jit(solution)/shard_map/ppermute | solution.py:54
  32.0 5.1 %collective-permute-start.7 = (f32[136,128]{1,0:T(8,128)S(1)}, f32[136,128]{1,0:T(8,128)S(1)}, u32[]{:S(2)}, u32[]{:S(2)}) collective-permute-start(f32[136,128]{1,0:T(8,128)S(1)} %get-tuple-element.38), channel_id=1, source_target_pairs={{0,13},{1,4},{2,15},{3,6},{4,1},{5,8},{6,3},{7,10},{8,5},{9,12},{1... | collective-permute-start | bytes 208904 | tf_op jit(solution)/shard_map/ppermute | solution.py:54
  32.0 6.5 %collective-permute-start.8 = (f32[136,128]{1,0:T(8,128)S(1)}, f32[136,128]{1,0:T(8,128)S(1)}, u32[]{:S(2)}, u32[]{:S(2)}) collective-permute-start(f32[136,128]{1,0:T(8,128)S(1)} %get-tuple-element.39), channel_id=1, source_target_pairs={{0,15},{1,14},{2,5},{3,4},{4,3},{5,2},{6,9},{7,8},{8,7},{9,6},{10,... | collective-permute-start | bytes 208904 | tf_op jit(solution)/shard_map/ppermute | solution.py:54
  35.0 3.5 %collective-permute-start.9 = (f32[136,128]{1,0:T(8,128)S(1)}, f32[136,128]{1,0:T(8,128)S(1)}, u32[]{:S(2)}, u32[]{:S(2)}) collective-permute-start(f32[136,128]{1,0:T(8,128)S(1)} %get-tuple-element.40), channel_id=1, source_target_pairs={{0,1},{1,0},{2,3},{3,2},{4,5},{5,4},{6,7},{7,6},{8,9},{9,8},{10,11... | collective-permute-start | bytes 208904 | tf_op jit(solution)/shard_map/ppermute | solution.py:54
  35.0 5.3 %collective-permute-start.10 = (f32[136,128]{1,0:T(8,128)S(1)}, f32[136,128]{1,0:T(8,128)S(1)}, u32[]{:S(2)}, u32[]{:S(2)}) collective-permute-start(f32[136,128]{1,0:T(8,128)S(1)} %get-tuple-element.41), channel_id=1, source_target_pairs={{0,2},{1,3},{2,0},{3,1},{4,6},{5,7},{6,4},{7,5},{8,10},{9,11},{10,... | collective-permute-start | bytes 208904 | tf_op jit(solution)/shard_map/ppermute | solution.py:54
  35.5 6.4 %collective-permute-start.11 = (f32[136,128]{1,0:T(8,128)S(1)}, f32[136,128]{1,0:T(8,128)S(1)}, u32[]{:S(2)}, u32[]{:S(2)}) collective-permute-start(f32[136,128]{1,0:T(8,128)S(1)} %get-tuple-element.42), channel_id=1, source_target_pairs={{0,3},{1,2},{2,1},{3,0},{4,7},{5,6},{6,5},{7,4},{8,11},{9,10},{10,... | collective-permute-start | bytes 208904 | tf_op jit(solution)/shard_map/ppermute | solution.py:54

commit v4 on v3

--- a/solution.py
+++ b/solution.py
@@ -10,6 +10,7 @@
 GROUP = 4
 ROWS = 8
 PARTS = 4
+CHUNK = 4
 TILE = 16
 VMEM_LIMIT = 24 << 20
 F32 = jnp.float32
@@ -33,7 +34,7 @@
         plans.append(far)
     for mask in range(1, group):
         plans.append([(k ^ mask) - k for k in range(group)])
-    plans = [plans[k] for k in (2, 1, 0, 3, 4, 5)]
+    plans = [plans[k] for k in (2, 1, 0, 4, 5, 3)]
     return [
         ([(i, (i + far[i % group]) % length) for i in range(length)], far) for far in plans
     ]
@@ -111,16 +112,18 @@
     size, offset, modes, eigen, row_offset, coupling, turned, offsets, inverse, *rest
 ):
     packed = rest[:NEAR]
-    rows, values, wants, blocks_in, span_rows, picked, sums, arrived = rest[NEAR:]
+    rows, values, wants, blocks_in, span_rows, chosen, picked, sums, arrived = rest[NEAR:]
     blocks, picks, width = coupling.shape
     span = span_rows.shape[0]
-    part = rows.shape[0] // PARTS
-    pairs = [(row_offset, wants), (offset, offsets), (eigen, values)]
-    pairs += [
-        (modes.at[pl.ds(k * part, part), :], rows.at[pl.ds(k * part, part), :])
-        for k in range(PARTS)
-    ]
-    pairs.append((coupling, blocks_in))
+    start = size[0] - span
+    base = jnp.minimum(start // TILE * TILE, modes.shape[0] - span - TILE)
+    part = -(-(span + TILE) // (PARTS * TILE)) * TILE
+    pairs = [(row_offset, wants), (eigen, values)]
+    for first in range(0, span + TILE, part):
+        some = min(part, span + TILE - first)
+        source = modes.at[pl.ds(pl.multiple_of(base + first, TILE), some), :]
+        pairs.append((source, rows.at[pl.ds(first, some), :]))
+    pairs += [(offset, offsets), (coupling, blocks_in)]
     copies = [
         pltpu.make_async_copy(source, target, arrived.at[k])
         for k, (source, target) in enumerate(pairs)
@@ -129,17 +132,23 @@
         copy.start()
     sums[...] = jnp.zeros_like(sums)
     _, place = iotas((picks, span))
-    for copy in copies[:3]:
+    copies[0].wait()
+    wanted = (span - 1 - wants[...]).T
+
+    def choose(i):
+        return jnp.concatenate(
+            [
+                jnp.where(place == wanted[:, b : b + 1], 1.0, 0.0).astype(BF16)
+                for b in range(i * GROUP, (i + 1) * GROUP)
+            ],
+            axis=0,
+        )
+
+    for copy in copies[1:-2]:
         copy.wait()
-    wanted = (span - 1 - wants[...]).T
     inverse[...] = 1.0 / values[...]
     weight = inverse[...] * inverse[...]
-    start = size[0] - span
-    base = jnp.minimum(start // TILE * TILE, rows.shape[0] - span - TILE)
-    for copy in copies[3:]:
-        copy.wait()
-    window = rows[pl.ds(pl.multiple_of(base, TILE), span + TILE), :].astype(F32)
-    moved = pltpu.roll(window, span + TILE - (start - base), 0)
+    moved = pltpu.roll(rows[...].astype(F32), span + TILE - (start - base), 0)
     span_rows[...] = moved[:span].astype(BF16)
     groups = blocks // GROUP
     for i in range(groups + 2):
@@ -155,11 +164,11 @@
                 mine = picked[(i - 1) % 2, g * picks : (g + 1) * picks, :]
                 turned[b] = dot(blocks_in[b].T, mine).astype(BF16)
         if i < groups:
-            chosen = [
-                jnp.where(place == wanted[:, b : b + 1], 1.0, 0.0).astype(BF16)
-                for b in range(i * GROUP, (i + 1) * GROUP)
-            ]
-            picked[i % 2] = dot(jnp.concatenate(chosen, axis=0), span_rows[...]).astype(BF16)
+            rows_of = choose(i)
+            picked[i % 2] = dot(rows_of, span_rows[...]).astype(BF16)
+        if i == 0:
+            for copy in copies[-2:]:
+                copy.wait()
     half = width // 2
     for message, slot in zip(packed, slots() + [REACH], strict=True):
         message[:half, :], message[half:, :] = pack(sums[slot])
@@ -273,13 +282,13 @@
         upper = upper + jnp.where(row < column, piece, 0.0)
         diagonal = diagonal + parcel[width : width + 1, :]
     copies = []
-    for first in range(0, blocks, GROUP):
-        for b in range(first, first + GROUP):
+    for first in range(0, blocks, CHUNK):
+        for b in range(first, first + CHUNK):
             twice = jnp.concatenate([projected[b], projected[b]], axis=1)
             held[b] = dot(twice, split[offset[b]], (1, 1)).astype(BF16)
-        some = pl.ds(first, GROUP)
+        some = pl.ds(first, CHUNK)
         copies.append(
-            pltpu.make_async_copy(held.at[some], coupled.at[some], sent.at[first // GROUP])
+            pltpu.make_async_copy(held.at[some], coupled.at[some], sent.at[first // CHUNK])
         )
         copies[-1].start()
     on_diagonal = jnp.where(row == column, diagonal, 0.0)
@@ -320,11 +329,12 @@
         ]
         + [near(width // 2 + ROWS, width)] * NEAR,
         scratch_shapes=[
-            pltpu.VMEM(modes.shape, BF16),
+            pltpu.VMEM((span + TILE, kept), BF16),
             pltpu.VMEM(eigenvalues.shape, F32),
             pltpu.VMEM(row_offset.shape, jnp.int32),
             pltpu.VMEM(stiff_coupling.shape, BF16),
             pltpu.VMEM((span, kept), BF16),
+            pltpu.VMEM((GROUP * picks, span), BF16),
             pltpu.VMEM((2, GROUP * picks, kept), BF16),
             pltpu.VMEM((NEAR, width, width), F32),
             pltpu.SemaphoreType.DMA((4 + PARTS,)),
@@ -365,7 +375,7 @@
         scratch_shapes=[
             pltpu.VMEM((NEAR, width, 2 * width), BF16),
             pltpu.VMEM((blocks, kept, width), BF16),
-            pltpu.SemaphoreType.DMA((blocks // GROUP,)),
+            pltpu.SemaphoreType.DMA((blocks // CHUNK,)),
         ],
         compiler_params=pltpu.CompilerParams(vmem_limit_bytes=VMEM_LIMIT),
         name="transform",

time: 46.5 us -> 44.9 us (0.966)
  waiting for transfers between devices: 5.87 us -> 3.74 us
  starting transfers between devices: 16.3 us -> 17.4 us
  Pallas kernels: 22.2 us -> 21.7 us
    ppermute x12, waiting for transfers between devices: 5.87 us -> 3.74 us  [exchanged(): lax.ppermute(x, 'sub', pairs)]
    ppermute x12, starting transfers between devices: 16.3 us -> 17.4 us  [exchanged(): lax.ppermute(x, 'sub', pairs)]
    pallas_call x1, Pallas kernels: 11.1 us -> 10.6 us  [per_device(): pl.pallas_call(project_kernel, in_specs=[in_smem()] + [pl.BlockSpec(memor...]
  transfers between devices with their start and end apart: 12 -> 12, of which waited for: 5 -> 3; matrix products, arithmetic and copies ran while one was open for 0% -> 0% of each run, Pallas kernels for 6% -> 6%
where the time goes in v4:
time: 44.9 us; the launch traced here: 44.5 us
  Pallas kernels  21.7 us (48%)
  starting transfers between devices  17.4 us (39%)
  waiting for transfers between devices  3.74 us (8%)
  between operations  1.54 us (3%)
    ppermute x12, starting transfers between devices, exchanged(): lax.ppermute(x, 'sub', pairs)  17.4 us
    pallas_call x1, Pallas kernels, per_device(): pl.pallas_call(project_kernel, in_specs=[in_smem()] + [pl.BlockSpec(memor...  10.6 us
    pallas_call x1, Pallas kernels, per_device(): pl.pallas_call(factor_kernel, in_specs=[in_vmem()] * (NEAR + 2), out_spec...  4.53 us
    pallas_call x1, Pallas kernels, per_device(): pl.pallas_call(transform_kernel, in_specs=[in_smem()] + [in_vmem()] * (NE...  3.95 us
    ppermute x12, waiting for transfers between devices, exchanged(): lax.ppermute(x, 'sub', pairs)  3.74 us
    pallas_call x1, Pallas kernels, per_device(): pl.pallas_call(stiffen_kernel, in_specs=[in_smem()] + [in_vmem()] * 2, ou...  2.65 us
  transfers between devices with their start and end apart: 12, of which 3 were waited for; matrix products, arithmetic and copies ran while one was open for 0% of the time, Pallas kernels for 6%

profile of v4, /device:TPU:1, one launch (start us, length us, event | category | flops | bytes accessed | tf_op | source)
XLA Modules:
  0.0 44.5 jit_solution(12602617387006344204)
XLA Ops:
  0.6 0.0 copy-start.1
  0.6 0.0 copy-start
  1.3 10.6 %project.1 = (bf16[32,128,512]{2,1,0:T(8,128)(2,1)S(1)}, s32[32]{0:T(128)S(4)}, f32[1,512]{1,0:T(1,128)S(1)}, f32[72,128]{1,0:T(8,128)S(1)}, f32[72,128]{1,0:T(8...) custom-call(s32[1]{0:T(128)S(6)} %copy.11.size, ...), custom_call_target="tpu_custom_call" | custom-call | tf_op jit(solution)/shard_map/project/pallas_call | solution.py:321
  11.9 5.1 %collective-permute-start = (f32[72,128]{1,0:T(8,128)S(1)}, f32[72,128]{1,0:T(8,128)S(1)}, u32[]{:S(2)}, u32[]{:S(2)}) collective-permute-start(f32[72,128]{1,0:T(8,128)S(1)} %get-tuple-element.29), channel_id=1, source_target_pairs={{0,14},{1,15},{2,4},{3,5},{4,2},{5,3},{6,8},{7,9},{8,6},{9,7},{10,... | collective-permute-start | bytes 110600 | tf_op jit(solution)/shard_map/ppermute | solution.py:55
  17.1 0.0 collective-permute-start.1
  17.1 1.7 %collective-permute-start.2 = (f32[72,128]{1,0:T(8,128)S(1)}, f32[72,128]{1,0:T(8,128)S(1)}, u32[]{:S(2)}, u32[]{:S(2)}) collective-permute-start(f32[72,128]{1,0:T(8,128)S(1)} %get-tuple-element.31), channel_id=1, source_target_pairs={{0,15},{1,14},{2,5},{3,4},{4,3},{5,2},{6,9},{7,8},{8,7},{9,6},{10,... | collective-permute-start | bytes 110600 | tf_op jit(solution)/shard_map/ppermute | solution.py:55
  18.8 1.2 %collective-permute-start.3 = (f32[72,128]{1,0:T(8,128)S(1)}, f32[72,128]{1,0:T(8,128)S(1)}, u32[]{:S(2)}, u32[]{:S(2)}) collective-permute-start(f32[72,128]{1,0:T(8,128)S(1)} %get-tuple-element.32), channel_id=1, source_target_pairs={{0,2},{1,3},{2,0},{3,1},{4,6},{5,7},{6,4},{7,5},{8,10},{9,11},{10,... | collective-permute-start | bytes 110600 | tf_op jit(solution)/shard_map/ppermute | solution.py:55
  20.0 1.1 %collective-permute-start.4 = (f32[72,128]{1,0:T(8,128)S(1)}, f32[72,128]{1,0:T(8,128)S(1)}, u32[]{:S(2)}, u32[]{:S(2)}) collective-permute-start(f32[72,128]{1,0:T(8,128)S(1)} %get-tuple-element.33), channel_id=1, source_target_pairs={{0,3},{1,2},{2,1},{3,0},{4,7},{5,6},{6,5},{7,4},{8,11},{9,10},{10,... | collective-permute-start | bytes 110600 | tf_op jit(solution)/shard_map/ppermute | solution.py:55
  21.2 0.0 collective-permute-done.refs_0_
  21.2 0.0 collective-permute-start.5
  21.2 2.7 %stiffen.1 = (bf16[32,512,128]{2,1,0:T(8,128)(2,1)S(1)}, f32[7,128,128]{2,1,0:T(8,128)S(1)}) custom-call(s32[32]{0:T(128)S(4)} %get-tuple-element.25.offset, f32[1,512]{1,0:T(1,128)S(1)} %get-tuple-element.26.inverse, bf16[32,128,512]{2,1,0:T(8,128)(2,1)S(1)} %get-tuple-element.27.turned), custom_call_target="tpu_custom_call" | custom-call | tf_op jit(solution)/shard_map/stiffen/pallas_call | solution.py:353
  23.8 0.0 collective-permute-done.1.refs_1_
  23.8 0.0 collective-permute-done.2.refs_2_
  23.8 0.0 collective-permute-done.3.refs_3_
  23.9 0.1 collective-permute-done.4.refs_4_
  24.0 0.0 collective-permute-done.5.refs_5_
  24.0 0.0 copy-done.1
  24.0 4.5 %factor.1 = (f32[1,128,128]{2,1,0:T(8,128)}, f32[136,128]{1,0:T(8,128)S(1)}, f32[136,128]{1,0:T(8,128)S(1)}, f32[136,128]{1,0:T(8,128)S(1)}, f32[136,128]{1,0:T(...) custom-call(f32[72,128]{1,0:T(8,128)S(1)} %collective-permute-done.refs_0_, ...), custom_call_target="tpu_custom_call" | custom-call | tf_op jit(solution)/shard_map/factor/pallas_call | solution.py:361
  28.5 3.2 %collective-permute-start.6 = (f32[136,128]{1,0:T(8,128)S(1)}, f32[136,128]{1,0:T(8,128)S(1)}, u32[]{:S(2)}, u32[]{:S(2)}) collective-permute-start(f32[136,128]{1,0:T(8,128)S(1)} %get-tuple-element.37), channel_id=1, source_target_pairs={{0,14},{1,15},{2,4},{3,5},{4,2},{5,3},{6,8},{7,9},{8,6},{9,7},{10,... | collective-permute-start | bytes 208904 | tf_op jit(solution)/shard_map/ppermute | solution.py:55
  31.7 0.0 collective-permute-start.7
  31.7 1.6 %collective-permute-start.8 = (f32[136,128]{1,0:T(8,128)S(1)}, f32[136,128]{1,0:T(8,128)S(1)}, u32[]{:S(2)}, u32[]{:S(2)}) collective-permute-start(f32[136,128]{1,0:T(8,128)S(1)} %get-tuple-element.39), channel_id=1, source_target_pairs={{0,15},{1,14},{2,5},{3,4},{4,3},{5,2},{6,9},{7,8},{8,7},{9,6},{10,... | collective-permute-start | bytes 208904 | tf_op jit(solution)/shard_map/ppermute | solution.py:55
  33.3 1.3 %collective-permute-start.9 = (f32[136,128]{1,0:T(8,128)S(1)}, f32[136,128]{1,0:T(8,128)S(1)}, u32[]{:S(2)}, u32[]{:S(2)}) collective-permute-start(f32[136,128]{1,0:T(8,128)S(1)} %get-tuple-element.40), channel_id=1, source_target_pairs={{0,2},{1,3},{2,0},{3,1},{4,6},{5,7},{6,4},{7,5},{8,10},{9,11},{10,... | collective-permute-start | bytes 208904 | tf_op jit(solution)/shard_map/ppermute | solution.py:55
  34.6 0.6 %collective-permute-start.10 = (f32[136,128]{1,0:T(8,128)S(1)}, f32[136,128]{1,0:T(8,128)S(1)}, u32[]{:S(2)}, u32[]{:S(2)}) collective-permute-start(f32[136,128]{1,0:T(8,128)S(1)} %get-tuple-element.41), channel_id=1, source_target_pairs={{0,3},{1,2},{2,1},{3,0},{4,7},{5,6},{6,5},{7,4},{8,11},{9,10},{10,... | collective-permute-start | bytes 208904 | tf_op jit(solution)/shard_map/ppermute | solution.py:55
  35.2 0.0 collective-permute-done.6.refs_0_
  35.2 1.6 %collective-permute-start.11 = (f32[136,128]{1,0:T(8,128)S(1)}, f32[136,128]{1,0:T(8,128)S(1)}, u32[]{:S(2)}, u32[]{:S(2)}) collective-permute-start(f32[136,128]{1,0:T(8,128)S(1)} %get-tuple-element.42), channel_id=1, source_target_pairs={{0,1},{1,0},{2,3},{3,2},{4,5},{5,4},{6,7},{7,6},{8,9},{9,8},{10,11... | collective-permute-start | bytes 208904 | tf_op jit(solution)/shard_map/ppermute | solution.py:55
  36.8 0.0 collective-permute-done.7.refs_1_
  36.8 1.4 %collective-permute-done.8.refs_2_ = f32[136,128]{1,0:T(8,128)S(1)} collective-permute-done((f32[136,128]{1,0:T(8,128)S(1)}, f32[136,128]{1,0:T(8,128)S(1)}, u32[]{:S(2)}, u32[]{:S(2)}) %collective-permute-start.8) | collective-permute-done | bytes 69664 | tf_op jit(solution)/shard_map/ppermute | solution.py:55
  38.2 0.0 collective-permute-done.9.refs_3_
  38.2 2.2 %collective-permute-done.10.refs_4_ = f32[136,128]{1,0:T(8,128)S(1)} collective-permute-done((f32[136,128]{1,0:T(8,128)S(1)}, f32[136,128]{1,0:T(8,128)S(1)}, u32[]{:S(2)}, u32[]{:S(2)}) %collective-permute-start.10) | collective-permute-done | bytes 69664 | tf_op jit(solution)/shard_map/ppermute | solution.py:55
  40.4 0.0 collective-permute-done.11.refs_5_
  40.4 0.0 copy-done
  40.4 4.0 %transform.1 = (f32[1,128,128]{2,1,0:T(8,128)}, bf16[32,512,128]{2,1,0:T(8,128)(2,1)}) custom-call(s32[32]{0:T(128)S(4)} %get-tuple-element.25.offset, bf16[32,512,128]{2,1,0:T(8,128)(2,1)S(1)} %get-tuple-element.28.projected, f32[1,128,128]{2,1,0:T(8,128)S(1)} %copy-done, f32[136,128]{1,0:T(8,128)S(1)} %collective-permute-done.6.refs_0_, ...), custom_call_target="tpu_custom_call" | custom-call | tf_op jit(solution)/shard_map/transform/pallas_call | solution.py:370
Async XLA Ops:
  0.6 23.3 %copy-start.1 = (f32[1,128]{1,0:T(1,128)S(1)}, f32[1,128]{1,0:T(1,128)}, u32[]{:S(2)}) copy-start(f32[1,128]{1,0:T(1,128)} %refs_7_.1) | copy-start | bytes 1540
  0.6 39.7 %copy-start = (f32[1,128,128]{2,1,0:T(8,128)S(1)}, f32[1,128,128]{2,1,0:T(8,128)}, u32[]{:S(2)}) copy-start(f32[1,128,128]{2,1,0:T(8,128)} %stiff_iface.1) | copy-start | bytes 196612
  11.9 9.2 %collective-permute-start = (f32[72,128]{1,0:T(8,128)S(1)}, f32[72,128]{1,0:T(8,128)S(1)}, u32[]{:S(2)}, u32[]{:S(2)}) collective-permute-start(f32[72,128]{1,0:T(8,128)S(1)} %get-tuple-element.29), channel_id=1, source_target_pairs={{0,14},{1,15},{2,4},{3,5},{4,2},{5,3},{6,8},{7,9},{8,6},{9,7},{10,... | collective-permute-start | bytes 110600 | tf_op jit(solution)/shard_map/ppermute | solution.py:55
  17.1 6.7 %collective-permute-start.1 = (f32[72,128]{1,0:T(8,128)S(1)}, f32[72,128]{1,0:T(8,128)S(1)}, u32[]{:S(2)}, u32[]{:S(2)}) collective-permute-start(f32[72,128]{1,0:T(8,128)S(1)} %get-tuple-element.30), channel_id=1, source_target_pairs={{0,13},{1,4},{2,15},{3,6},{4,1},{5,8},{6,3},{7,10},{8,5},{9,12},{1... | collective-permute-start | bytes 110600 | tf_op jit(solution)/shard_map/ppermute | solution.py:55
  17.1 6.8 %collective-permute-start.2 = (f32[72,128]{1,0:T(8,128)S(1)}, f32[72,128]{1,0:T(8,128)S(1)}, u32[]{:S(2)}, u32[]{:S(2)}) collective-permute-start(f32[72,128]{1,0:T(8,128)S(1)} %get-tuple-element.31), channel_id=1, source_target_pairs={{0,15},{1,14},{2,5},{3,4},{4,3},{5,2},{6,9},{7,8},{8,7},{9,6},{10,... | collective-permute-start | bytes 110600 | tf_op jit(solution)/shard_map/ppermute | solution.py:55
  18.8 5.1 %collective-permute-start.3 = (f32[72,128]{1,0:T(8,128)S(1)}, f32[72,128]{1,0:T(8,128)S(1)}, u32[]{:S(2)}, u32[]{:S(2)}) collective-permute-start(f32[72,128]{1,0:T(8,128)S(1)} %get-tuple-element.32), channel_id=1, source_target_pairs={{0,2},{1,3},{2,0},{3,1},{4,6},{5,7},{6,4},{7,5},{8,10},{9,11},{10,... | collective-permute-start | bytes 110600 | tf_op jit(solution)/shard_map/ppermute | solution.py:55
  20.0 4.0 %collective-permute-start.4 = (f32[72,128]{1,0:T(8,128)S(1)}, f32[72,128]{1,0:T(8,128)S(1)}, u32[]{:S(2)}, u32[]{:S(2)}) collective-permute-start(f32[72,128]{1,0:T(8,128)S(1)} %get-tuple-element.33), channel_id=1, source_target_pairs={{0,3},{1,2},{2,1},{3,0},{4,7},{5,6},{6,5},{7,4},{8,11},{9,10},{10,... | collective-permute-start | bytes 110600 | tf_op jit(solution)/shard_map/ppermute | solution.py:55
  21.2 2.8 %collective-permute-start.5 = (f32[72,128]{1,0:T(8,128)S(1)}, f32[72,128]{1,0:T(8,128)S(1)}, u32[]{:S(2)}, u32[]{:S(2)}) collective-permute-start(f32[72,128]{1,0:T(8,128)S(1)} %get-tuple-element.34), channel_id=1, source_target_pairs={{0,1},{1,0},{2,3},{3,2},{4,5},{5,4},{6,7},{7,6},{8,9},{9,8},{10,11... | collective-permute-start | bytes 110600 | tf_op jit(solution)/shard_map/ppermute | solution.py:55
  28.5 6.7 %collective-permute-start.6 = (f32[136,128]{1,0:T(8,128)S(1)}, f32[136,128]{1,0:T(8,128)S(1)}, u32[]{:S(2)}, u32[]{:S(2)}) collective-permute-start(f32[136,128]{1,0:T(8,128)S(1)} %get-tuple-element.37), channel_id=1, source_target_pairs={{0,14},{1,15},{2,4},{3,5},{4,2},{5,3},{6,8},{7,9},{8,6},{9,7},{10,... | collective-permute-start | bytes 208904 | tf_op jit(solution)/shard_map/ppermute | solution.py:55
  31.7 5.1 %collective-permute-start.7 = (f32[136,128]{1,0:T(8,128)S(1)}, f32[136,128]{1,0:T(8,128)S(1)}, u32[]{:S(2)}, u32[]{:S(2)}) collective-permute-start(f32[136,128]{1,0:T(8,128)S(1)} %get-tuple-element.38), channel_id=1, source_target_pairs={{0,13},{1,4},{2,15},{3,6},{4,1},{5,8},{6,3},{7,10},{8,5},{9,12},{1... | collective-permute-start | bytes 208904 | tf_op jit(solution)/shard_map/ppermute | solution.py:55
  31.7 6.5 %collective-permute-start.8 = (f32[136,128]{1,0:T(8,128)S(1)}, f32[136,128]{1,0:T(8,128)S(1)}, u32[]{:S(2)}, u32[]{:S(2)}) collective-permute-start(f32[136,128]{1,0:T(8,128)S(1)} %get-tuple-element.39), channel_id=1, source_target_pairs={{0,15},{1,14},{2,5},{3,4},{4,3},{5,2},{6,9},{7,8},{8,7},{9,6},{10,... | collective-permute-start | bytes 208904 | tf_op jit(solution)/shard_map/ppermute | solution.py:55
  33.3 4.9 %collective-permute-start.9 = (f32[136,128]{1,0:T(8,128)S(1)}, f32[136,128]{1,0:T(8,128)S(1)}, u32[]{:S(2)}, u32[]{:S(2)}) collective-permute-start(f32[136,128]{1,0:T(8,128)S(1)} %get-tuple-element.40), channel_id=1, source_target_pairs={{0,2},{1,3},{2,0},{3,1},{4,6},{5,7},{6,4},{7,5},{8,10},{9,11},{10,... | collective-permute-start | bytes 208904 | tf_op jit(solution)/shard_map/ppermute | solution.py:55
  34.6 5.8 %collective-permute-start.10 = (f32[136,128]{1,0:T(8,128)S(1)}, f32[136,128]{1,0:T(8,128)S(1)}, u32[]{:S(2)}, u32[]{:S(2)}) collective-permute-start(f32[136,128]{1,0:T(8,128)S(1)} %get-tuple-element.41), channel_id=1, source_target_pairs={{0,3},{1,2},{2,1},{3,0},{4,7},{5,6},{6,5},{7,4},{8,11},{9,10},{10,... | collective-permute-start | bytes 208904 | tf_op jit(solution)/shard_map/ppermute | solution.py:55
  35.2 5.2 %collective-permute-start.11 = (f32[136,128]{1,0:T(8,128)S(1)}, f32[136,128]{1,0:T(8,128)S(1)}, u32[]{:S(2)}, u32[]{:S(2)}) collective-permute-start(f32[136,128]{1,0:T(8,128)S(1)} %get-tuple-element.42), channel_id=1, source_target_pairs={{0,1},{1,0},{2,3},{3,2},{4,5},{5,4},{6,7},{7,6},{8,9},{9,8},{10,11... | collective-permute-start | bytes 208904 | tf_op jit(solution)/shard_map/ppermute | solution.py:55
